TPU v7x, 32 devices: a whole 2x2x4 slice. The times are simulated.
32 devices in a mesh: seq: 8 (over z, x), head: 4 (over y, core).
Axes of the slice: x: 2, y: 2, z: 4, core: 2. Of those that a mesh axis runs over, the one named last changes fastest.
Arguments:
- block_order: int32 [16], replicated, may hold values from 0 to 15, each once
- queries: bfloat16 [2048, 4096], P('seq', 'head'), may hold values from -52 to 52
- keys: bfloat16 [2048, 4096], P('seq', 'head'), may hold values from -4.5 to 4.5
- values: bfloat16 [2048, 4096], P('seq', 'head'), may hold values from -5 to 5
- hyena_q: bfloat16 [2048, 4096], P('seq', 'head'), may hold values from -5 to 5
- hyena_k: bfloat16 [2048, 4096], P('seq', 'head'), may hold values from -5 to 5
- hyena_v: bfloat16 [2048, 4096], P('seq', 'head'), may hold values from -5 to 5
- hyena_grad: bfloat16 [2048, 4096], P('seq', 'head'), may hold values from -5 to 5
- filters: float32 [256, 128], P('head'), may hold values from -0.5 to 0.5
- proj_weight: bfloat16 [3, 4096, 4096], P(None, None, 'head'), may hold values from -0.0546875 to 0.0546875
Outputs:
- input_grad: bfloat16 [2048, 4096], P('seq', 'head')
- query_grad: bfloat16 [2048, 4096], P('seq', 'head')
- key_grad: bfloat16 [2048, 4096], P('seq', 'head')
- value_grad: bfloat16 [2048, 4096], P('seq', 'head')
Inputs may be any that keep to these rules, and one draw needn't show every extreme that they name: `block_order`: A permutation of the sequence blocks; entry 2 d + j is the position block of rows d * 256 + j * 128 to d * 256 + j * 128 + 127.
All inputs are finite; a program needn't handle non-finite values.
Results may differ from a plain program's by a relative error of at most 0.01.
Values may be sent and summed in bfloat16 or wider, within the bound.
A program may use at most 128 MiB of HBM per device.

v0:
```python
import functools

import jax
import jax.numpy as jnp
from jax import lax
from jax.experimental import pallas as pl
from jax.experimental.pallas import tpu as pltpu
from jax.sharding import PartitionSpec as P

HD = 128
GROUP = 16
KL = 128
BLOCK = 128


def for_sending(x):

    def short(part):
        return part.astype(jnp.bfloat16) if part.dtype == jnp.float32 else part

    return jax.tree.map(short, x)


def passed_along(value, axis, steps):
    count = lax.axis_size(axis)
    pairs = [(source, (source + steps) % count) for source in range(count)]
    return lax.ppermute(value, axis, pairs)


def keep_state(current):
    return current


def ring_device(
    block_order, queries, keys, values, hyena_q, hyena_k, hyena_v, hyena_grad, filters, proj_weight
):
    seq_count = lax.axis_size("seq")
    my_index = lax.axis_index("seq")
    row_count = queries.shape[0]
    feature_width = queries.shape[1]
    head_count = feature_width // HD
    block_total = block_order.shape[0]
    offsets = jnp.arange(BLOCK, dtype=jnp.int32)
    block_ids = jnp.arange(block_total, dtype=jnp.int32)

    def block_positions(source):
        block_pair = lax.dynamic_slice_in_dim(block_order, 2 * source, 2)
        return jnp.concatenate([block_pair[0] * BLOCK + offsets, block_pair[1] * BLOCK + offsets])

    def holder_of(target):
        return jnp.sum(jnp.where(block_order == target, block_ids, 0))

    my_positions = block_positions(my_index)
    product_kv = (hyena_k.astype(jnp.float32) * hyena_v.astype(jnp.float32)).astype(jnp.bfloat16)
    product_dq = (hyena_grad.astype(jnp.float32) * hyena_q.astype(jnp.float32)).astype(jnp.bfloat16)
    my_blocks = [
        lax.dynamic_index_in_dim(block_order, 2 * my_index + portion, 0, keepdims=False)
        for portion in range(2)
    ]
    gathered_z, gathered_dc = (
        lax.all_gather(product_kv, "seq", axis=0, tiled=True),
        lax.all_gather(product_dq, "seq", axis=0, tiled=True),
    )
    group_count = filters.shape[0]
    channels = hyena_q.shape[1]
    out_rows = jnp.arange(BLOCK)[:, None, None]
    window_rows = jnp.arange(BLOCK + KL)[None, :, None]
    tap_ids = jnp.arange(KL)[None, None, :]
    causal_table = (out_rows + KL - window_rows == tap_ids).astype(jnp.float32)
    anti_table = (window_rows - out_rows == tap_ids).astype(jnp.float32)
    causal_toeplitz = jnp.einsum(
        "gj,tsj->gts", filters, causal_table, precision=lax.Precision.HIGHEST
    )
    anti_toeplitz = jnp.einsum("gj,tsj->gts", filters, anti_table, precision=lax.Precision.HIGHEST)

    def apply_groups(toeplitz, window):
        grouped = window.astype(jnp.float32).reshape(BLOCK + KL, group_count, GROUP)
        result = jnp.einsum("gts,sgk->tgk", toeplitz, grouped, precision=lax.Precision.HIGHEST)
        return result.reshape(BLOCK, channels)

    conv_parts = []
    back_parts = []
    for portion in range(2):
        block_id = my_blocks[portion]
        before = lax.dynamic_slice_in_dim(
            gathered_z, holder_of(block_id - 1) * BLOCK + BLOCK - KL, KL, 0
        )
        before = jnp.where(block_id >= 1, before, jnp.zeros_like(before))
        after = lax.dynamic_slice_in_dim(gathered_dc, holder_of(block_id + 1) * BLOCK, KL, 0)
        after = jnp.where(block_id + 1 < block_total, after, jnp.zeros_like(after))
        own_z = product_kv[portion * BLOCK : (portion + 1) * BLOCK]
        own_dc = product_dq[portion * BLOCK : (portion + 1) * BLOCK]
        conv_parts.append(apply_groups(causal_toeplitz, jnp.concatenate([before, own_z])))
        back_parts.append(apply_groups(anti_toeplitz, jnp.concatenate([own_dc, after])))
    convolved = jnp.concatenate(conv_parts)
    back_conv = jnp.concatenate(back_parts)
    stacked = jnp.stack(
        [
            hyena_grad.astype(jnp.float32) * convolved,
            back_conv * hyena_v.astype(jnp.float32),
            back_conv * hyena_k.astype(jnp.float32),
        ]
    ).astype(jnp.bfloat16)
    summed = lax.psum_scatter(
        jnp.einsum("mic,mtc->it", proj_weight, stacked, preferred_element_type=jnp.float32),
        "head",
        scatter_dimension=0,
        tiled=True,
    )
    input_grad = summed.T.astype(jnp.bfloat16)
    score_scale = HD ** (-0.5)
    query_heads = queries.reshape(row_count, head_count, HD)
    key_heads = keys.reshape(row_count, head_count, HD)
    value_heads = values.reshape(row_count, head_count, HD)
    grad_heads = input_grad.reshape(row_count, head_count, HD)

    def tile_scores(query_block, key_block, query_pos, key_pos):
        scores = (
            jnp.einsum("qhd,khd->hqk", query_block, key_block, preferred_element_type=jnp.float32)
            * score_scale
        )
        allowed = (key_pos[None, :] <= query_pos[:, None])[None]
        return (scores, allowed)

    def stat_update(running, key_block, value_block, source):
        key_pos = block_positions(source)
        active = jnp.min(key_pos) <= jnp.max(my_positions)

        def stat_accumulate(current):
            row_max, row_sum, row_dot = current
            scores, allowed = tile_scores(query_heads, key_block, my_positions, key_pos)
            masked = jnp.where(allowed, scores, -1e30)
            new_max = jnp.maximum(row_max, jnp.max(masked, axis=2))
            terms = jnp.where(allowed, jnp.exp(masked - new_max[:, :, None]), 0.0)
            prob_grad = jnp.einsum(
                "qhd,khd->hqk", grad_heads, value_block, preferred_element_type=jnp.float32
            )
            factor = jnp.exp(row_max - new_max)
            return (
                new_max,
                row_sum * factor + jnp.sum(terms, axis=2),
                row_dot * factor + jnp.sum(terms * prob_grad, axis=2),
            )

        return lax.cond(active, stat_accumulate, keep_state, running)

    initial = (
        jnp.full((head_count, row_count), -1e30, jnp.float32),
        jnp.zeros((head_count, row_count), jnp.float32),
        jnp.zeros((head_count, row_count), jnp.float32),
    )

    def tile_grads(
        query_block, grad_block, norm_block, delta_block, query_pos, key_block, value_block, key_pos
    ):
        scores, allowed = tile_scores(query_block, key_block, query_pos, key_pos)
        probabilities = jnp.where(allowed, jnp.exp(scores - norm_block[:, :, None]), 0.0)
        prob_grad = jnp.einsum(
            "qhd,khd->hqk", grad_block, value_block, preferred_element_type=jnp.float32
        )
        score_grad = probabilities * (prob_grad - delta_block[:, :, None])
        probs_low = probabilities.astype(jnp.bfloat16)
        score_low = score_grad.astype(jnp.bfloat16)
        add_query = (
            jnp.einsum("hqk,khd->qhd", score_low, key_block, preferred_element_type=jnp.float32)
            * score_scale
        )
        add_key = (
            jnp.einsum("hqk,qhd->khd", score_low, query_block, preferred_element_type=jnp.float32)
            * score_scale
        )
        add_value = jnp.einsum(
            "hqk,qhd->khd", probs_low, grad_block, preferred_element_type=jnp.float32
        )
        return (add_query, add_key, add_value)

    zero_rows = jnp.zeros((row_count, head_count, HD), jnp.float32)

    def move_stat_queries(pair):
        return jax.tree.map(
            lambda part, own: part.astype(own.dtype),
            passed_along(for_sending(pair), "seq", 1),
            pair,
        )

    def stat_turn(turn_index, loop_state):
        running, key_block, value_block = loop_state
        source = (my_index - turn_index) % seq_count
        running = stat_update(running, key_block, value_block, source)
        key_block, value_block = move_stat_queries((key_block, value_block))
        return (running, key_block, value_block)

    loop_state = lax.fori_loop(0, seq_count - 1, stat_turn, (initial, key_heads, value_heads))
    running = stat_update(
        loop_state[0], loop_state[1], loop_state[2], (my_index - (seq_count - 1)) % seq_count
    )
    log_norm = running[0] + jnp.log(running[1])
    row_delta = running[2] / running[1]

    def query_turn(turn_index, loop_state):
        query_block, grad_block, norm_block, delta_block, query_acc, key_acc, value_acc = loop_state
        source = (my_index - turn_index) % seq_count
        query_pos = block_positions(source)
        active = jnp.min(my_positions) <= jnp.max(query_pos)

        def query_accumulate(current):
            add_query, add_key, add_value = tile_grads(
                query_block,
                grad_block,
                norm_block,
                delta_block,
                query_pos,
                key_heads,
                value_heads,
                my_positions,
            )
            return (current[0] + add_query, current[1] + add_key, current[2] + add_value)

        query_acc, key_acc, value_acc = lax.cond(
            active, query_accumulate, keep_state, (query_acc, key_acc, value_acc)
        )
        query_block, grad_block = passed_along((query_block, grad_block), "seq", 1)
        norm_block, delta_block, query_acc = passed_along(
            (norm_block, delta_block, query_acc), "seq", 1
        )
        return (query_block, grad_block, norm_block, delta_block, query_acc, key_acc, value_acc)

    final_state = lax.fori_loop(
        0,
        seq_count,
        query_turn,
        (query_heads, grad_heads, log_norm, row_delta, zero_rows, zero_rows, zero_rows),
    )
    query_total = final_state[4]
    key_total = final_state[5]
    value_total = final_state[6]
    query_grad = query_total.reshape(row_count, feature_width).astype(jnp.bfloat16)
    key_grad = key_total.reshape(row_count, feature_width).astype(jnp.bfloat16)
    value_grad = value_total.reshape(row_count, feature_width).astype(jnp.bfloat16)
    return (input_grad, query_grad, key_grad, value_grad)


MESH = pl.DeviceIdType.MESH
VMEM_SPEC = pl.BlockSpec(memory_space=pltpu.VMEM)
SMEM_SPEC = pl.BlockSpec(memory_space=pltpu.SMEM)


def aligned(index, size):
    return pl.ds(pl.multiple_of(index * size, size), size)


def signal_peers(me, n, head_peers=()):
    barrier = pltpu.get_barrier_semaphore()
    for step in range(1, n):
        pl.semaphore_signal(
            barrier, inc=1, device_id={"seq": lax.rem(me + step, n)}, device_id_type=MESH
        )
    for peer in head_peers:
        pl.semaphore_signal(barrier, inc=1, device_id={"head": peer}, device_id_type=MESH)


def greet(me, n, head_peers=()):
    signal_peers(me, n, head_peers)
    pl.semaphore_wait(pltpu.get_barrier_semaphore(), n - 1 + len(head_peers))


def exchange(n, me, rows, send_sem, recv_sem, own_sem):
    def parts(to_columns, src, dst, peer):
        if to_columns:
            return src.at[:, aligned(peer, HD)], dst.at[aligned(me, rows), :]
        return src.at[aligned(peer, rows), :], dst.at[:, aligned(me, HD)]

    def remote(tensor, to_columns, src, dst, step):
        peer = lax.rem(me + step, n)
        part, place = parts(to_columns, src, dst, peer)
        return pltpu.make_async_remote_copy(
            src_ref=part,
            dst_ref=place,
            send_sem=send_sem.at[tensor, step],
            recv_sem=recv_sem.at[tensor, step],
            device_id={"seq": peer},
            device_id_type=MESH,
        )

    def own(tensor, to_columns, src, dst):
        part, place = parts(to_columns, src, dst, me)
        return pltpu.make_async_copy(part, place, own_sem.at[tensor])

    def start(tensor, to_columns, src, dst):
        for step in range(1, n):
            remote(tensor, to_columns, src, dst, step).start()
        own(tensor, to_columns, src, dst).start()

    def wait(tensor, to_columns, src, dst):
        for step in range(1, n):
            remote(tensor, to_columns, src, dst, step).wait()
        own(tensor, to_columns, src, dst).wait()

    return remote, own, start, wait


def exchange_sems(tensors, n):
    return [
        pltpu.SemaphoreType.DMA((tensors, n)),
        pltpu.SemaphoreType.DMA((tensors, n)),
        pltpu.SemaphoreType.DMA((tensors,)),
    ]


def hyena_kernel(
    n, heads, groups,
    picks_ref, hq_ref, hk_ref, hv_ref, hg_ref, base_ref,
    q_ref, k_ref, v_ref, weight_ref,
    grad_ref, qc_ref, kc_ref, vc_ref, gc_ref,
    z_ref, dc_ref, conv_ref, dz_ref, zc, dcc, convc, dzc,
    causal_high, causal_low, anti_high, anti_low,
    stacked, weights, kept, pair_out, pair_in, line_out, line_in,
    send_sem, recv_sem, own_sem, weight_sem, pair_sem, line_sem,
):
    me = lax.axis_index("seq")
    head = lax.axis_index("head")
    rows, columns = z_ref.shape
    blocks = zc.shape[0] // BLOCK
    chips = heads // 2
    chip, core = head // 2, lax.rem(head, 2)
    partner = chip * 2 + 1 - core
    along = [lax.rem(chip + step, chips) for step in range(chips)]
    order = list(range(1, chips)) + [0]
    remote, own, start, wait = exchange(n, me, rows, send_sem, recv_sem, own_sem)

    def weight_copy(slot, goal, m):
        return pltpu.make_async_copy(
            weight_ref.at[m, aligned(goal, columns), :], weights.at[slot, m],
            weight_sem.at[slot, m],
        )

    for step in order:
        for mine in range(2):
            goal = along[step] * 2 + (core if mine else 1 - core)
            for m in range(3):
                weight_copy(2 * step + mine, goal, m).start()
    wide_of = lambda ref: ref[...].astype(jnp.float32)
    z_ref[...] = (wide_of(hk_ref) * wide_of(hv_ref)).astype(jnp.bfloat16)
    dc_ref[...] = (wide_of(hg_ref) * wide_of(hq_ref)).astype(jnp.bfloat16)
    greet(me, n, [partner] + [along[step] * 2 + core for step in range(1, chips)])
    start(0, True, z_ref, zc)
    start(1, True, dc_ref, dcc)

    window = 2 * BLOCK
    before_ref = picks_ref.at[: blocks * blocks, :]
    after_ref = picks_ref.at[blocks * blocks :, :]
    for at, high, low in ((0, causal_high, causal_low), (groups, anti_high, anti_low)):
        for g in range(groups):
            base = jnp.broadcast_to(base_ref[at + g : at + g + 1, :], (BLOCK, window))
            table = pltpu.roll(base, 0, 1, stride=1, stride_axis=0)
            top = table.astype(jnp.bfloat16)
            high[:, g * window : (g + 1) * window] = top
            low[:, g * window : (g + 1) * window] = (table - top.astype(jnp.float32)).astype(
                jnp.bfloat16
            )

    lane_group = lax.broadcasted_iota(jnp.int32, (window, 2 * HD), 1) % HD // GROUP

    def filtered(source, neighbours, high, low, target, place, own_first):
        halves = []
        for half in range(2):
            block = place * 2 + half
            own_rows = source[aligned(block, BLOCK), :]
            picks = neighbours[aligned(block, blocks), :]
            other = source[:BLOCK, :] * picks[0:1, :]
            for b in range(1, blocks):
                other = other + source[b * BLOCK : (b + 1) * BLOCK, :] * picks[b : b + 1, :]
            pair = [own_rows, other] if own_first else [other, own_rows]
            halves.append(jnp.concatenate(pair, axis=0))
        wide = jnp.concatenate(halves, axis=1)
        stack = jnp.concatenate(
            [jnp.where(lane_group == g, wide, jnp.zeros_like(wide)) for g in range(groups)], axis=0
        )
        result = jnp.dot(high[...], stack, preferred_element_type=jnp.float32)
        result = result + jnp.dot(low[...], stack, preferred_element_type=jnp.float32)
        result = result.astype(target.dtype)
        target[aligned(place, rows), :] = jnp.concatenate(
            [result[:, :HD], result[:, HD:]], axis=0
        )

    def send_back(tensor, source, neighbours, high, low, target, out, own_first):
        def one(step, carry):
            filtered(source, neighbours, high, low, target, lax.rem(me + step, n), own_first)
            remote(tensor, False, target, out, step).start()
            return carry

        lax.fori_loop(1, n, one, 0)
        filtered(source, neighbours, high, low, target, me, own_first)
        own(tensor, False, target, out).start()

    wait(0, True, z_ref, zc)
    send_back(2, zc, before_ref, causal_high, causal_low, convc, conv_ref, False)
    wait(1, True, dc_ref, dcc)
    send_back(3, dcc, after_ref, anti_high, anti_low, dzc, dz_ref, True)
    attention = ((4, q_ref, qc_ref), (5, k_ref, kc_ref), (6, v_ref, vc_ref))
    for t, src, dst in attention:
        start(t, True, src, dst)
    wait(2, False, convc, conv_ref)
    stacked[0] = (wide_of(hg_ref) * wide_of(conv_ref)).astype(jnp.bfloat16)
    wait(3, False, dzc, dz_ref)
    stacked[1] = (wide_of(dz_ref) * wide_of(hv_ref)).astype(jnp.bfloat16)
    stacked[2] = (wide_of(dz_ref) * wide_of(hk_ref)).astype(jnp.bfloat16)

    def project(slot, goal, target):
        for m in range(3):
            weight_copy(slot, goal, m).wait()
        tile = 2 * BLOCK

        def one(j, carry):
            total = None
            for m in range(3):
                part = lax.dot_general(
                    stacked[m], weights[slot, m, aligned(j, tile), :],
                    (((1,), (1,)), ((), ())), preferred_element_type=jnp.float32,
                )
                total = part if total is None else total + part
            target[:, aligned(j, tile)] = total
            return carry

        lax.fori_loop(0, columns // tile, one, 0)

    def pair_copy(step):
        return pltpu.make_async_remote_copy(
            src_ref=pair_out.at[step], dst_ref=pair_in.at[step],
            send_sem=pair_sem.at[0, step], recv_sem=pair_sem.at[1, step],
            device_id={"head": partner}, device_id_type=MESH,
        )

    def line_copy(step):
        return pltpu.make_async_remote_copy(
            src_ref=line_out.at[step - 1], dst_ref=line_in.at[step - 1],
            send_sem=line_sem.at[0, step], recv_sem=line_sem.at[1, step],
            device_id={"head": along[step] * 2 + core}, device_id_type=MESH,
        )

    for step in order:
        project(2 * step, along[step] * 2 + 1 - core, pair_out.at[step])
        pair_copy(step).start()
        project(2 * step + 1, along[step] * 2 + core, kept)
        pair_copy(step).wait()
        if step:
            line_out[step - 1] = kept[...] + pair_in[step]
            line_copy(step).start()
    total = kept[...] + pair_in[0]
    for step in range(1, chips):
        line_copy(step).wait()
        total = total + line_in[step - 1]
    grad_ref[...] = total.astype(grad_ref.dtype)
    start(7, True, grad_ref, gc_ref)
    for t, src, dst in attention:
        wait(t, True, src, dst)
    wait(7, True, grad_ref, gc_ref)


def hyena(
    n, heads, picks, hyena_q, hyena_k, hyena_v, hyena_grad, bases,
    queries, keys, values, proj_weight,
):
    rows, columns = queries.shape
    groups = bases.shape[0] // 2
    chips = heads // 2
    like = jax.ShapeDtypeStruct(queries.shape, jnp.bfloat16)
    moved = jax.ShapeDtypeStruct((rows * n, HD), jnp.bfloat16)
    table = pltpu.VMEM((BLOCK, groups * 2 * BLOCK), jnp.bfloat16)
    low = pltpu.VMEM((rows, columns), jnp.bfloat16)
    partial = lambda count: pltpu.VMEM((count, rows, columns), jnp.float32)
    return pl.pallas_call(
        functools.partial(hyena_kernel, n, heads, groups),
        out_shape=[like] + [moved] * 4,
        in_specs=[VMEM_SPEC] * 9 + [pl.BlockSpec(memory_space=pl.ANY)],
        out_specs=[VMEM_SPEC] * 5,
        scratch_shapes=[low] * 4
        + [pltpu.VMEM((rows * n, HD), jnp.bfloat16)] * 4
        + [table] * 4
        + [
            pltpu.VMEM((3, rows, columns), jnp.bfloat16),
            pltpu.VMEM((heads, 3, columns, columns), jnp.bfloat16),
            pltpu.VMEM((rows, columns), jnp.float32),
            partial(chips), partial(chips), partial(chips - 1), partial(chips - 1),
        ]
        + exchange_sems(8, n)
        + [
            pltpu.SemaphoreType.DMA((heads, 3)),
            pltpu.SemaphoreType.DMA((2, chips)),
            pltpu.SemaphoreType.DMA((2, chips)),
        ],
        compiler_params=pltpu.CompilerParams(
            collective_id=0, has_side_effects=True, vmem_limit_bytes=60 * 2**20
        ),
    )(
        picks, hyena_q, hyena_k, hyena_v, hyena_grad, bases,
        queries, keys, values, proj_weight,
    )


def attention_kernel(
    n, order_ref, holder_ref, q_ref, k_ref, v_ref, g_ref, dq_ref, dk_ref, dv_ref,
    ks, vs, kst, prob, dq_sum, dk_sum, dv_sum, dq_low, dk_low, dv_low, send_sem, recv_sem, own_sem,
):
    me = lax.axis_index("seq")
    blocks = order_ref.shape[0]
    _, _, start, wait = exchange(n, me, dq_ref.shape[0], send_sem, recv_sem, own_sem)
    signal_peers(me, n)
    scale = HD ** (-0.5)
    tile = 2 * BLOCK
    contract_last = (((1,), (1,)), ((), ()))
    for b in range(blocks):
        here = slice(b * BLOCK, (b + 1) * BLOCK)
        rows = k_ref[holder_ref[b]]
        ks[here, :] = rows
        kst[:, here] = rows.T
        vs[here, :] = v_ref[holder_ref[b]]

    def pair(ref, i):
        return jnp.concatenate([ref[holder_ref[2 * i]], ref[holder_ref[2 * i + 1]]], axis=0)

    def add(total, value, i):
        value = value.reshape(2 * i + 2, BLOCK, HD)
        if i == blocks // 2 - 1:
            total[...] = value
        else:
            total[: 2 * i + 2] += value

    def stored(i):
        return slice(tile * i * (i + 1) // 2, tile * (i + 1) * (i + 2) // 2)

    def give(total, factor, low):
        for s in range(blocks):
            rows = total[order_ref[s]]
            rows = rows if factor is None else rows * factor
            low[s * BLOCK : (s + 1) * BLOCK, :] = rows.astype(low.dtype)

    for i in reversed(range(blocks // 2)):
        width = (i + 1) * tile
        q = pair(q_ref, i)
        scores = lax.dot_general(
            ks[:width, :], q, contract_last, preferred_element_type=jnp.float32
        ) * scale
        key_at = lax.broadcasted_iota(jnp.int32, (tile, tile), 0)
        query_at = lax.broadcasted_iota(jnp.int32, (tile, tile), 1)
        last = jnp.where(key_at <= query_at, scores[width - tile :], -1e30)
        scores = jnp.concatenate([scores[: width - tile], last], axis=0) if i else last
        terms = jnp.exp(scores - jnp.max(scores, axis=0, keepdims=True))
        chance = terms * (1.0 / jnp.sum(terms, axis=0, keepdims=True))
        prob[stored(i), :] = chance
        add(
            dv_sum,
            jnp.dot(chance.astype(jnp.bfloat16), pair(g_ref, i), preferred_element_type=jnp.float32),
            i,
        )
    give(dv_sum, None, dv_low)
    pl.semaphore_wait(pltpu.get_barrier_semaphore(), n - 1)
    start(0, False, dv_low, dv_ref)
    for i in reversed(range(blocks // 2)):
        width = (i + 1) * tile
        prob_grad = lax.dot_general(
            vs[:width, :], pair(g_ref, i), contract_last, preferred_element_type=jnp.float32
        )
        chance = prob[stored(i), :]
        delta = jnp.sum(chance * prob_grad, axis=0, keepdims=True)
        score_grad = (chance * (prob_grad - delta)).astype(jnp.bfloat16)
        add(
            dk_sum,
            jnp.dot(score_grad, pair(q_ref, i), preferred_element_type=jnp.float32),
            i,
        )
        query_t = jnp.dot(kst[:, :width], score_grad, preferred_element_type=jnp.float32)
        dq_sum[2 * i : 2 * i + 2] = (query_t.T * scale).reshape(2, BLOCK, HD)
    give(dq_sum, None, dq_low)
    start(1, False, dq_low, dq_ref)
    give(dk_sum, scale, dk_low)
    start(2, False, dk_low, dk_ref)
    wait(0, False, dv_low, dv_ref)
    wait(1, False, dq_low, dq_ref)
    wait(2, False, dk_low, dk_ref)


def attention(n, order, holder, *tensors):
    rows = tensors[0].shape[0]
    blocks = rows // BLOCK
    low = pltpu.VMEM((rows, HD), jnp.bfloat16)
    full = pltpu.VMEM((blocks, BLOCK, HD), jnp.float32)
    tiles = rows // (2 * BLOCK)
    stored = 2 * BLOCK * tiles * (tiles + 1) // 2
    return pl.pallas_call(
        functools.partial(attention_kernel, n),
        out_shape=[jax.ShapeDtypeStruct((rows // n, HD * n), jnp.bfloat16)] * 3,
        in_specs=[SMEM_SPEC] * 2 + [VMEM_SPEC] * 4,
        out_specs=[VMEM_SPEC] * 3,
        scratch_shapes=[low, low, pltpu.VMEM((HD, rows), jnp.bfloat16)]
        + [pltpu.VMEM((stored, 2 * BLOCK), jnp.float32)]
        + [full] * 3
        + [low] * 3
        + exchange_sems(3, n),
        compiler_params=pltpu.CompilerParams(
            collective_id=1, has_side_effects=True, vmem_limit_bytes=50 * 2**20
        ),
    )(order, holder, *[t.reshape(blocks, BLOCK, HD) for t in tensors])


def land_kernel(count, *refs):
    for source, target in zip(refs[:count], refs[count:]):
        target[...] = source[...]


def land(*arrays):
    count = len(arrays)
    return pl.pallas_call(
        functools.partial(land_kernel, count),
        out_shape=[jax.ShapeDtypeStruct(a.shape, a.dtype) for a in arrays],
        in_specs=[VMEM_SPEC] * count,
        out_specs=[VMEM_SPEC] * count,
    )(*arrays)


def column_device(
    block_order, queries, keys, values, hyena_q, hyena_k, hyena_v, hyena_grad, filters, proj_weight
):
    n = lax.axis_size("seq")
    me = lax.axis_index("seq")
    blocks = block_order.shape[0]
    ids = jnp.arange(blocks, dtype=jnp.int32)
    holder = jnp.sum(
        jnp.where(block_order[None, :] == ids[:, None], ids[None, :], 0), axis=1
    ).astype(jnp.int32)

    wanted = jnp.concatenate([block_order - 1, block_order + 1])
    found = wanted[:, None, None] == block_order[None, :, None]
    picks = jnp.broadcast_to(found, (2 * blocks, blocks, HD)).astype(jnp.bfloat16)
    picks = picks.reshape(2 * blocks * blocks, HD)
    groups = filters.shape[0] // n
    taps = lax.dynamic_slice_in_dim(filters, me * groups, groups, 0)
    gap = jnp.zeros((groups, 1), taps.dtype)
    bases = jnp.concatenate(
        [
            jnp.concatenate([gap, taps[:, ::-1], jnp.zeros((groups, KL - 1), taps.dtype)], axis=1),
            jnp.concatenate([taps, jnp.zeros_like(taps)], axis=1),
        ],
        axis=0,
    )
    heads = lax.axis_size("head")
    input_grad, qc, kc, vc, gc = hyena(
        n, heads, picks, hyena_q, hyena_k, hyena_v, hyena_grad, bases, queries, keys, values, proj_weight,
    )
    grads = attention(n, block_order, holder, qc, kc, vc, gc)
    return tuple(land(input_grad, *grads))


def per_device(*arrays):
    queries, filters = arrays[1], arrays[8]
    n = lax.axis_size("seq")
    whole_heads = queries.shape[1] == n * HD and queries.shape[0] == 2 * BLOCK
    paired = lax.axis_size("head") % 2 == 0 and lax.axis_size("head") > 2
    if whole_heads and paired and filters.shape[0] % n == 0 and KL == BLOCK == HD:
        return column_device(*arrays)
    return ring_device(*arrays)


def solution(mesh):
    placed = (
        P(),
        P("seq", "head"),
        P("seq", "head"),
        P("seq", "head"),
        P("seq", "head"),
        P("seq", "head"),
        P("seq", "head"),
        P("seq", "head"),
        P("head", None),
        P(None, None, "head"),
    )
    return jax.shard_map(
        per_device,
        mesh=mesh,
        in_specs=placed,
        out_specs=(P("seq", "head"), P("seq", "head"), P("seq", "head"), P("seq", "head")),
        check_vma=False,
    )
```

profile of v0, /device:TPU:0, one launch (start us, length us, event | category | flops | bytes accessed | tf_op | source)
XLA Modules:
  0.0 169.4 jit_solution(11576503665033740658)
XLA Ops:
  0.6 0.0 copy-start
  0.6 0.0 copy-start.8
  0.7 0.8 select_reduce_fusion.holder_ref
  1.5 0.7 broadcast_add_fusion.1
  2.2 0.1 pad_add_fusion
  2.2 0.0 copy-done
  2.2 0.1 rev.3
  2.3 0.7 select_maximum_fusion.base_ref
  3.0 0.1 eq.36
  3.1 0.1 eq.37
  3.1 0.7 eq.38
  3.8 0.1 eq.39
  3.9 0.8 broadcast_in_dim.16.picks_ref
  4.7 112.0 %shard_map.129 = (bf16[256,1024]{1,0:T(8,128)(2,1)}, bf16[2048,128]{1,0:T(8,128)(2,1)}, bf16[2048,128]{1,0:T(8,128)(2,1)}, bf16[2048,128]{1,0:T(8,128)(2,1)}, bf16[2048,128]{1,0:T(8,128)(2,1)}) custom-call(bf16[512,128]{1,0:T(8,128)(2,1)} %broadcast_in_dim.16.picks_ref, bf16[256,1024]{1,0:T(8,128)(2,1)} %hq_ref.1, bf16[256,1024]{1,0:T(8,128)(2,1)} %hk_ref.1, ...), custom_call_target="tpu_custom_call" | custom-call | tf_op jit(solution)/shard_map/pallas_call | solution.py:472
  116.7 0.0 copy-done.8
  116.7 0.0 copy-start.4
  116.7 1.0 copy-done.4
  117.8 0.0 copy-start.5
  117.8 1.0 copy-done.5
  118.8 0.0 copy-start.6
  118.8 1.0 copy-done.6
  119.8 0.0 copy-start.7
  119.8 1.0 copy-done.7
  120.9 43.3 %shard_map.130 = (bf16[256,1024]{1,0:T(8,128)(2,1)S(1)}, bf16[256,1024]{1,0:T(8,128)(2,1)S(1)}, bf16[256,1024]{1,0:T(8,128)(2,1)S(1)}) custom-call(s32[16]{0:T(128)S(1)} %copy-done.8, s32[16]{0:T(128)S(1)} %select_reduce_fusion.holder_ref, bf16[16,128,128]{2,1,0:T(8,128)(2,1)S(1)} %bitcast.6, bf16[16,128,128]{2,1,0:T(8,128)(2,1)S(1)} %bitcast.7, ...), custom_call_target="tpu_custom_call" | custom-call | tf_op jit(solution)/shard_map/pallas_call | solution.py:590
  164.2 0.0 copy-start.1
  164.2 0.8 copy-done.1
  164.9 0.0 copy-start.2
  164.9 0.8 copy-done.2
  165.8 0.0 copy-start.3
  165.8 0.8 copy-done.3
  166.6 2.9 %shard_map.131 = (bf16[256,1024]{1,0:T(8,128)(2,1)}, bf16[256,1024]{1,0:T(8,128)(2,1)}, bf16[256,1024]{1,0:T(8,128)(2,1)}, bf16[256,1024]{1,0:T(8,128)(2,1)}) custom-call(bf16[256,1024]{1,0:T(8,128)(2,1)} %get-tuple-element.12.refs_0_, bf16[256,1024]{1,0:T(8,128)(2,1)} %copy-done.1, bf16[256,1024]{1,0:T(8,128)(2,1)} %copy-done.2, bf16[256,1024]{1,0:T(8,128)(2,1)} %copy-done.3), custom_call_target="tpu_custom_call" | custom-call | tf_op jit(solution)/shard_map/pallas_call | solution.py:613
  (4 shorter events, 0.0 us)
Async XLA Ops:
  0.6 1.6 copy-start
  0.6 116.1 %copy-start.8 = (s32[16]{0:T(128)S(1)}, s32[16]{0:T(128)}, u32[]{:S(2)}) copy-start(s32[16]{0:T(128)} %order_ref.1) | copy-start | bytes 196
  116.7 1.0 copy-start.4
  117.8 1.0 copy-start.5
  118.8 1.0 copy-start.6
  119.8 1.0 copy-start.7
  164.2 0.8 copy-start.1
  164.9 0.8 copy-start.2
  165.8 0.8 copy-start.3
where the time goes:
time: 170 us; the launch traced here: 169 us
  Pallas kernels  158 us (93%)
  local copies, waits for them, and re-layouts  8.32 us (5%)
  other arithmetic  2.25 us (1%)
    pallas_call x1, Pallas kernels, hyena(): pl.pallas_call(functools.partial(hyena_kernel, n, heads, groups), out_sha...  112 us
    pallas_call x1, Pallas kernels, attention(): pl.pallas_call(functools.partial(attention_kernel, n), out_shape=[jax.Sha...  43.3 us
    unnamed x18, local copies, waits for them, and re-layouts  6.55 us

commit v1 on v0

v1 whole, which is shorter than its diff:
```python
import functools

import jax
import jax.numpy as jnp
from jax import lax
from jax.experimental import pallas as pl
from jax.experimental.pallas import tpu as pltpu
from jax.sharding import PartitionSpec as P

HD = 128
GROUP = 16
KL = 128
BLOCK = 128


def for_sending(x):

    def short(part):
        return part.astype(jnp.bfloat16) if part.dtype == jnp.float32 else part

    return jax.tree.map(short, x)


def passed_along(value, axis, steps):
    count = lax.axis_size(axis)
    pairs = [(source, (source + steps) % count) for source in range(count)]
    return lax.ppermute(value, axis, pairs)


def keep_state(current):
    return current


def ring_device(
    block_order, queries, keys, values, hyena_q, hyena_k, hyena_v, hyena_grad, filters, proj_weight
):
    seq_count = lax.axis_size("seq")
    my_index = lax.axis_index("seq")
    row_count = queries.shape[0]
    feature_width = queries.shape[1]
    head_count = feature_width // HD
    block_total = block_order.shape[0]
    offsets = jnp.arange(BLOCK, dtype=jnp.int32)
    block_ids = jnp.arange(block_total, dtype=jnp.int32)

    def block_positions(source):
        block_pair = lax.dynamic_slice_in_dim(block_order, 2 * source, 2)
        return jnp.concatenate([block_pair[0] * BLOCK + offsets, block_pair[1] * BLOCK + offsets])

    def holder_of(target):
        return jnp.sum(jnp.where(block_order == target, block_ids, 0))

    my_positions = block_positions(my_index)
    product_kv = (hyena_k.astype(jnp.float32) * hyena_v.astype(jnp.float32)).astype(jnp.bfloat16)
    product_dq = (hyena_grad.astype(jnp.float32) * hyena_q.astype(jnp.float32)).astype(jnp.bfloat16)
    my_blocks = [
        lax.dynamic_index_in_dim(block_order, 2 * my_index + portion, 0, keepdims=False)
        for portion in range(2)
    ]
    gathered_z, gathered_dc = (
        lax.all_gather(product_kv, "seq", axis=0, tiled=True),
        lax.all_gather(product_dq, "seq", axis=0, tiled=True),
    )
    group_count = filters.shape[0]
    channels = hyena_q.shape[1]
    out_rows = jnp.arange(BLOCK)[:, None, None]
    window_rows = jnp.arange(BLOCK + KL)[None, :, None]
    tap_ids = jnp.arange(KL)[None, None, :]
    causal_table = (out_rows + KL - window_rows == tap_ids).astype(jnp.float32)
    anti_table = (window_rows - out_rows == tap_ids).astype(jnp.float32)
    causal_toeplitz = jnp.einsum(
        "gj,tsj->gts", filters, causal_table, precision=lax.Precision.HIGHEST
    )
    anti_toeplitz = jnp.einsum("gj,tsj->gts", filters, anti_table, precision=lax.Precision.HIGHEST)

    def apply_groups(toeplitz, window):
        grouped = window.astype(jnp.float32).reshape(BLOCK + KL, group_count, GROUP)
        result = jnp.einsum("gts,sgk->tgk", toeplitz, grouped, precision=lax.Precision.HIGHEST)
        return result.reshape(BLOCK, channels)

    conv_parts = []
    back_parts = []
    for portion in range(2):
        block_id = my_blocks[portion]
        before = lax.dynamic_slice_in_dim(
            gathered_z, holder_of(block_id - 1) * BLOCK + BLOCK - KL, KL, 0
        )
        before = jnp.where(block_id >= 1, before, jnp.zeros_like(before))
        after = lax.dynamic_slice_in_dim(gathered_dc, holder_of(block_id + 1) * BLOCK, KL, 0)
        after = jnp.where(block_id + 1 < block_total, after, jnp.zeros_like(after))
        own_z = product_kv[portion * BLOCK : (portion + 1) * BLOCK]
        own_dc = product_dq[portion * BLOCK : (portion + 1) * BLOCK]
        conv_parts.append(apply_groups(causal_toeplitz, jnp.concatenate([before, own_z])))
        back_parts.append(apply_groups(anti_toeplitz, jnp.concatenate([own_dc, after])))
    convolved = jnp.concatenate(conv_parts)
    back_conv = jnp.concatenate(back_parts)
    stacked = jnp.stack(
        [
            hyena_grad.astype(jnp.float32) * convolved,
            back_conv * hyena_v.astype(jnp.float32),
            back_conv * hyena_k.astype(jnp.float32),
        ]
    ).astype(jnp.bfloat16)
    summed = lax.psum_scatter(
        jnp.einsum("mic,mtc->it", proj_weight, stacked, preferred_element_type=jnp.float32),
        "head",
        scatter_dimension=0,
        tiled=True,
    )
    input_grad = summed.T.astype(jnp.bfloat16)
    score_scale = HD ** (-0.5)
    query_heads = queries.reshape(row_count, head_count, HD)
    key_heads = keys.reshape(row_count, head_count, HD)
    value_heads = values.reshape(row_count, head_count, HD)
    grad_heads = input_grad.reshape(row_count, head_count, HD)

    def tile_scores(query_block, key_block, query_pos, key_pos):
        scores = (
            jnp.einsum("qhd,khd->hqk", query_block, key_block, preferred_element_type=jnp.float32)
            * score_scale
        )
        allowed = (key_pos[None, :] <= query_pos[:, None])[None]
        return (scores, allowed)

    def stat_update(running, key_block, value_block, source):
        key_pos = block_positions(source)
        active = jnp.min(key_pos) <= jnp.max(my_positions)

        def stat_accumulate(current):
            row_max, row_sum, row_dot = current
            scores, allowed = tile_scores(query_heads, key_block, my_positions, key_pos)
            masked = jnp.where(allowed, scores, -1e30)
            new_max = jnp.maximum(row_max, jnp.max(masked, axis=2))
            terms = jnp.where(allowed, jnp.exp(masked - new_max[:, :, None]), 0.0)
            prob_grad = jnp.einsum(
                "qhd,khd->hqk", grad_heads, value_block, preferred_element_type=jnp.float32
            )
            factor = jnp.exp(row_max - new_max)
            return (
                new_max,
                row_sum * factor + jnp.sum(terms, axis=2),
                row_dot * factor + jnp.sum(terms * prob_grad, axis=2),
            )

        return lax.cond(active, stat_accumulate, keep_state, running)

    initial = (
        jnp.full((head_count, row_count), -1e30, jnp.float32),
        jnp.zeros((head_count, row_count), jnp.float32),
        jnp.zeros((head_count, row_count), jnp.float32),
    )

    def tile_grads(
        query_block, grad_block, norm_block, delta_block, query_pos, key_block, value_block, key_pos
    ):
        scores, allowed = tile_scores(query_block, key_block, query_pos, key_pos)
        probabilities = jnp.where(allowed, jnp.exp(scores - norm_block[:, :, None]), 0.0)
        prob_grad = jnp.einsum(
            "qhd,khd->hqk", grad_block, value_block, preferred_element_type=jnp.float32
        )
        score_grad = probabilities * (prob_grad - delta_block[:, :, None])
        probs_low = probabilities.astype(jnp.bfloat16)
        score_low = score_grad.astype(jnp.bfloat16)
        add_query = (
            jnp.einsum("hqk,khd->qhd", score_low, key_block, preferred_element_type=jnp.float32)
            * score_scale
        )
        add_key = (
            jnp.einsum("hqk,qhd->khd", score_low, query_block, preferred_element_type=jnp.float32)
            * score_scale
        )
        add_value = jnp.einsum(
            "hqk,qhd->khd", probs_low, grad_block, preferred_element_type=jnp.float32
        )
        return (add_query, add_key, add_value)

    zero_rows = jnp.zeros((row_count, head_count, HD), jnp.float32)

    def move_stat_queries(pair):
        return jax.tree.map(
            lambda part, own: part.astype(own.dtype),
            passed_along(for_sending(pair), "seq", 1),
            pair,
        )

    def stat_turn(turn_index, loop_state):
        running, key_block, value_block = loop_state
        source = (my_index - turn_index) % seq_count
        running = stat_update(running, key_block, value_block, source)
        key_block, value_block = move_stat_queries((key_block, value_block))
        return (running, key_block, value_block)

    loop_state = lax.fori_loop(0, seq_count - 1, stat_turn, (initial, key_heads, value_heads))
    running = stat_update(
        loop_state[0], loop_state[1], loop_state[2], (my_index - (seq_count - 1)) % seq_count
    )
    log_norm = running[0] + jnp.log(running[1])
    row_delta = running[2] / running[1]

    def query_turn(turn_index, loop_state):
        query_block, grad_block, norm_block, delta_block, query_acc, key_acc, value_acc = loop_state
        source = (my_index - turn_index) % seq_count
        query_pos = block_positions(source)
        active = jnp.min(my_positions) <= jnp.max(query_pos)

        def query_accumulate(current):
            add_query, add_key, add_value = tile_grads(
                query_block,
                grad_block,
                norm_block,
                delta_block,
                query_pos,
                key_heads,
                value_heads,
                my_positions,
            )
            return (current[0] + add_query, current[1] + add_key, current[2] + add_value)

        query_acc, key_acc, value_acc = lax.cond(
            active, query_accumulate, keep_state, (query_acc, key_acc, value_acc)
        )
        query_block, grad_block = passed_along((query_block, grad_block), "seq", 1)
        norm_block, delta_block, query_acc = passed_along(
            (norm_block, delta_block, query_acc), "seq", 1
        )
        return (query_block, grad_block, norm_block, delta_block, query_acc, key_acc, value_acc)

    final_state = lax.fori_loop(
        0,
        seq_count,
        query_turn,
        (query_heads, grad_heads, log_norm, row_delta, zero_rows, zero_rows, zero_rows),
    )
    query_total = final_state[4]
    key_total = final_state[5]
    value_total = final_state[6]
    query_grad = query_total.reshape(row_count, feature_width).astype(jnp.bfloat16)
    key_grad = key_total.reshape(row_count, feature_width).astype(jnp.bfloat16)
    value_grad = value_total.reshape(row_count, feature_width).astype(jnp.bfloat16)
    return (input_grad, query_grad, key_grad, value_grad)


MESH = pl.DeviceIdType.MESH
VMEM_SPEC = pl.BlockSpec(memory_space=pltpu.VMEM)
ANY_SPEC = pl.BlockSpec(memory_space=pl.ANY)
SMEM_SPEC = pl.BlockSpec(memory_space=pltpu.SMEM)


def aligned(index, size):
    return pl.ds(pl.multiple_of(index * size, size), size)


def fused_kernel(
    n, heads, slots,
    order_ref, filters_ref, hq_in, hk_in, hv_in, hg_in, q_in, k_in, v_in, weight_in,
    grad_ref, dq_ref, dk_ref, dv_ref,
    hq, hk, hv, hg, qs, ks, vs, z_own, dc_own,
    zc, dcc, z_out, dc_out, z_far, dc_far,
    causal, anti, convc, dzc, conv, dz, stacked, weights,
    total, pair_in, line_out, line_in,
    qc, kc, vc, gc, keys, keys_t, values, prob, dq_sum, dk_sum, dv_sum, dq_low, dk_low, dv_low,
    holder, after, before, z_cross, dc_cross, z_rank, dc_rank, z_pick, dc_pick,
    load_sem, weight_sem, own_sem, send_sem, recv_sem,
    half_send, half_recv, half_own, far_send, far_recv, pair_sem, line_sem,
):
    me = lax.axis_index("seq")
    head = lax.axis_index("head")
    chips = heads // 2
    chip, core = head // 2, lax.rem(head, 2)
    partner = chip * 2 + 1 - core
    along = [lax.rem(chip + step, chips) for step in range(chips)]
    steps = list(range(1, chips)) + [0]
    blocks = order_ref.shape[0]
    members = n // 2
    held = blocks // 2
    side, place = me // members, lax.rem(me, members)
    base = side * held
    width = hq.shape[2]
    part = zc.shape[2]
    groups = part // GROUP
    tile = 2 * BLOCK
    tiles = width // tile

    loads = [
        pltpu.make_async_copy(source, target, load_sem.at[i])
        for i, (source, target) in enumerate(
            ((hg_in, hg), (hq_in, hq), (hk_in, hk), (hv_in, hv), (q_in, qs), (k_in, ks), (v_in, vs))
        )
    ]
    for copy in loads:
        copy.start()

    def weight_copy(m, slot):
        return pltpu.make_async_copy(weight_in.at[m], weights.at[slot], weight_sem.at[m])

    weight_copy(1, 0).start()
    weight_copy(2, 1).start()

    barrier = pltpu.get_barrier_semaphore()
    for step in range(1, n):
        pl.semaphore_signal(
            barrier, inc=1, device_id={"seq": lax.rem(me + step, n)}, device_id_type=MESH
        )
    head_peers = [partner] + [along[step] * 2 + core for step in range(1, chips)]
    for peer in head_peers:
        pl.semaphore_signal(barrier, inc=1, device_id={"head": peer}, device_id_type=MESH)

    def wide_of(ref):
        return ref[...].astype(jnp.float32)

    loads[0].wait()
    loads[1].wait()
    dc_own[...] = (wide_of(hg) * wide_of(hq)).astype(jnp.bfloat16)
    loads[2].wait()
    loads[3].wait()
    z_own[...] = (wide_of(hk) * wide_of(hv)).astype(jnp.bfloat16)
    pl.semaphore_wait(barrier, n - 1 + len(head_peers))

    def to_head(tensor, src, dst, step):
        peer = lax.rem(me + step, n)
        return pltpu.make_async_remote_copy(
            src_ref=src.at[:, :, aligned(peer, HD)], dst_ref=dst.at[aligned(me, 2)],
            send_sem=send_sem.at[tensor, step], recv_sem=recv_sem.at[tensor, step],
            device_id={"seq": peer}, device_id_type=MESH,
        )

    def to_rows(tensor, src, dst, step):
        peer = lax.rem(me + step, n)
        return pltpu.make_async_remote_copy(
            src_ref=src.at[aligned(peer, 2)], dst_ref=dst.at[:, :, aligned(me, HD)],
            send_sem=send_sem.at[tensor, step], recv_sem=recv_sem.at[tensor, step],
            device_id={"seq": peer}, device_id_type=MESH,
        )

    def own_head(tensor, src, dst):
        return pltpu.make_async_copy(
            src.at[:, :, aligned(me, HD)], dst.at[aligned(me, 2)], own_sem.at[tensor]
        )

    def own_rows(tensor, src, dst):
        return pltpu.make_async_copy(
            src.at[aligned(me, 2)], dst.at[:, :, aligned(me, HD)], own_sem.at[tensor]
        )

    def start_all(make, own, tensor, src, dst):
        for step in range(1, n):
            make(tensor, src, dst, step).start()
        own(tensor, src, dst).start()

    def wait_all(make, own, tensor, src, dst):
        for step in range(1, n):
            make(tensor, src, dst, step).wait()
        own(tensor, src, dst).wait()

    def spread(tensor, src, dst, step):
        goal = lax.rem(place + step, members)
        return pltpu.make_async_remote_copy(
            src_ref=src.at[:, :, aligned(goal, part)], dst_ref=dst.at[aligned(place, 2)],
            send_sem=half_send.at[tensor, step], recv_sem=half_recv.at[tensor, step],
            device_id={"seq": side * members + goal}, device_id_type=MESH,
        )

    def spread_own(tensor, src, dst):
        return pltpu.make_async_copy(
            src.at[:, :, aligned(place, part)], dst.at[aligned(place, 2)], half_own.at[tensor]
        )

    def collect(tensor, src, dst, step):
        goal = lax.rem(place + step, members)
        return pltpu.make_async_remote_copy(
            src_ref=src.at[aligned(goal, 2)], dst_ref=dst.at[:, :, aligned(place, part)],
            send_sem=half_send.at[tensor, step], recv_sem=half_recv.at[tensor, step],
            device_id={"seq": side * members + goal}, device_id_type=MESH,
        )

    def collect_own(tensor, src, dst):
        return pltpu.make_async_copy(
            src.at[aligned(place, 2)], dst.at[:, :, aligned(place, part)], half_own.at[tensor]
        )

    def cross(tensor, src, dst):
        return pltpu.make_async_remote_copy(
            src_ref=src, dst_ref=dst.at[pl.ds(0, slots)],
            send_sem=far_send.at[tensor], recv_sem=far_recv.at[tensor],
            device_id={"seq": lax.rem(me + members, n)}, device_id_type=MESH,
        )

    for tensor, src, dst in ((0, dc_own, dcc), (1, z_own, zc)):
        for step in range(1, members):
            spread(tensor, src, dst, step).start()
        spread_own(tensor, src, dst).start()

    order = [order_ref[r] for r in range(blocks)]
    for p in range(blocks):
        found = jnp.int32(0)
        for r in range(1, blocks):
            found = jnp.where(order[r] == p, r, found)
        holder[p] = found
    for start in (0, held):
        z_count, dc_count = jnp.int32(0), jnp.int32(0)
        for r in range(start, start + held):
            later = holder[jnp.minimum(order[r] + 1, blocks - 1)]
            later = jnp.where(order[r] + 1 < blocks, later, r)
            sooner = holder[jnp.maximum(order[r] - 1, 0)]
            sooner = jnp.where(order[r] > 0, sooner, r)
            leaves = (later < held) if start else (later >= held)
            returns = (sooner < held) if start else (sooner >= held)
            leaves = jnp.where(leaves, 1, 0)
            returns = jnp.where(returns, 1, 0)
            after[r], before[r] = later, sooner
            z_cross[r], dc_cross[r] = leaves, returns
            z_rank[r], dc_rank[r] = z_count, dc_count
            z_count, dc_count = z_count + leaves, dc_count + returns
    for pick, crossing, rank in ((dc_pick, dc_cross, dc_rank), (z_pick, z_cross, z_rank)):
        flags = [crossing[base + l] for l in range(held)]
        ranks = [rank[base + l] for l in range(held)]
        for k in range(slots):
            found = jnp.int32(0)
            for l in range(1, held):
                found = jnp.where((flags[l] == 1) & (ranks[l] == k), l, found)
            pick[k] = found

    window = 2 * BLOCK
    taps = filters_ref[aligned(place, groups), :]
    flip = jnp.where(
        lax.broadcasted_iota(jnp.int32, (KL, KL), 0) + lax.broadcasted_iota(jnp.int32, (KL, KL), 1)
        == KL - 1, 1.0, 0.0,
    ).astype(jnp.bfloat16)
    high = taps.astype(jnp.bfloat16)
    low = (taps - high.astype(jnp.float32)).astype(jnp.bfloat16)
    turned = jnp.dot(high, flip, preferred_element_type=jnp.float32)
    turned = turned + jnp.dot(low, flip, preferred_element_type=jnp.float32)
    for table, rows, shift in ((anti, taps, 0), (causal, turned, 1)):
        padded = jnp.concatenate([rows, jnp.zeros_like(rows)], axis=1)
        for g in range(groups):
            line = jnp.broadcast_to(padded[g : g + 1, :], (BLOCK, window))
            line = pltpu.roll(line, shift, 1, stride=1, stride_axis=0)
            top = line.astype(jnp.bfloat16)
            table[:BLOCK, g * window : (g + 1) * window] = top
            table[BLOCK:, g * window : (g + 1) * window] = (
                line - top.astype(jnp.float32)
            ).astype(jnp.bfloat16)

    for tensor, src, dst, pick, out, far in (
        (0, dc_own, dcc, dc_pick, dc_out, dc_far), (1, z_own, zc, z_pick, z_out, z_far)
    ):
        for step in range(1, members):
            spread(tensor, src, dst, step).wait()
        spread_own(tensor, src, dst).wait()
        for k in range(slots):
            out[k] = dst[pick[k]]
        cross(tensor, out, far).start()

    lane_group = lax.broadcasted_iota(jnp.int32, (window, window), 1) % HD // GROUP
    chunks = part // HD
    chunk_groups = groups // chunks

    def filtered(goal, near, far, linked, end, rank, table, target, own_first):
        pairs = []
        for half in range(2):
            local = goal * 2 + half
            row = base + local
            own = near[local]
            link = linked[row]
            inside = (link >= base) & (link < base + held)
            some = jnp.where(order_ref[row] == end, 0.0, 1.0)
            here = jnp.where(inside, some, 0.0)
            there = jnp.where(inside, 0.0, some)
            found = near[jnp.where(inside, link - base, 0)].astype(jnp.float32) * here
            sent = far[jnp.where(inside, 0, jnp.minimum(rank[link], slots - 1))]
            other = (found + sent.astype(jnp.float32) * there).astype(jnp.bfloat16)
            pairs.append((own, other) if own_first else (other, own))
        for c in range(chunks):
            lanes = slice(c * HD, (c + 1) * HD)
            wide = jnp.concatenate(
                [jnp.concatenate([a[:, lanes], b[:, lanes]], axis=0) for a, b in pairs], axis=1
            )
            stack = jnp.concatenate(
                [
                    jnp.where(lane_group == g, wide, jnp.zeros_like(wide))
                    for g in range(chunk_groups)
                ],
                axis=0,
            )
            span = chunk_groups * window
            result = jnp.dot(
                table[:, c * span : (c + 1) * span], stack, preferred_element_type=jnp.float32
            )
            result = (result[:BLOCK] + result[BLOCK:]).astype(target.dtype)
            target[goal * 2, :, lanes] = result[:, :HD]
            target[goal * 2 + 1, :, lanes] = result[:, HD:]

    def send_back(tensor, near, far, linked, end, rank, table, target, out, own_first):
        def one(step, carry):
            goal = lax.rem(place + step, members)
            filtered(goal, near, far, linked, end, rank, table, target, own_first)
            collect(tensor, target, out, step).start()
            return carry

        lax.fori_loop(1, members, one, 0)
        filtered(place, near, far, linked, end, rank, table, target, own_first)
        collect_own(tensor, target, out).start()

    def returned(tensor, target, out):
        for step in range(1, members):
            collect(tensor, target, out, step).wait()
        collect_own(tensor, target, out).wait()

    def rows_of(value):
        return value.reshape(tile, width)

    cross(0, dc_out, dc_far).wait()
    send_back(2, dcc, dc_far, after, blocks - 1, dc_rank, anti, dzc, dz, True)
    cross(1, z_out, z_far).wait()
    send_back(3, zc, z_far, before, 0, z_rank, causal, convc, conv, False)
    attention = ((0, qs, qc), (1, ks, kc), (2, vs, vc))
    for t, src, dst in attention:
        loads[4 + t].wait()
        start_all(to_head, own_head, t, src, dst)

    goals = []
    for step in steps:
        goals.append(along[step] * 2 + 1 - core)
        goals.append(along[step] * 2 + core)

    def product(m, slot, goal, j):
        return lax.dot_general(
            stacked[m], weights[slot, aligned(goal * tiles + j, tile), :],
            (((1,), (1,)), ((), ())), preferred_element_type=jnp.float32,
        )

    returned(2, dzc, dz)
    wide = wide_of(dz)
    stacked[1] = rows_of((wide * wide_of(hv)).astype(jnp.bfloat16))
    stacked[2] = rows_of((wide * wide_of(hk)).astype(jnp.bfloat16))
    weight_copy(1, 0).wait()
    weight_copy(2, 1).wait()
    for slot, goal in enumerate(goals):
        def begin(j, carry, slot=slot, goal=goal):
            total[slot, j] = product(1, 0, goal, j) + product(2, 1, goal, j)
            return carry

        lax.fori_loop(0, tiles, begin, 0)
    weight_copy(0, 0).start()
    returned(3, convc, conv)
    stacked[0] = rows_of((wide_of(hg) * wide_of(conv)).astype(jnp.bfloat16))
    weight_copy(0, 0).wait()

    def pair_copy(at, j):
        return pltpu.make_async_remote_copy(
            src_ref=total.at[2 * at, j], dst_ref=pair_in.at[at, j],
            send_sem=pair_sem.at[0, at, j], recv_sem=pair_sem.at[1, at, j],
            device_id={"head": partner}, device_id_type=MESH,
        )

    def line_copy(at, j):
        return pltpu.make_async_remote_copy(
            src_ref=line_out.at[at, j], dst_ref=line_in.at[at, j],
            send_sem=line_sem.at[0, at, j], recv_sem=line_sem.at[1, at, j],
            device_id={"head": along[steps[at]] * 2 + core}, device_id_type=MESH,
        )

    for at in range(chips):
        def give_pair(j, carry, at=at):
            total[2 * at, j] += product(0, 0, goals[2 * at], j)
            pair_copy(at, j).start()
            return carry

        lax.fori_loop(0, tiles, give_pair, 0)

        def keep(j, carry, at=at):
            value = total[2 * at + 1, j] + product(0, 0, goals[2 * at + 1], j)
            if at < chips - 1:
                pair_copy(at, j).wait()
                line_out[at, j] = (value + pair_in[at, j]).astype(line_out.dtype)
                line_copy(at, j).start()
            else:
                total[2 * at + 1, j] = value
            return carry

        lax.fori_loop(0, tiles, keep, 0)
    last = chips - 1
    for j in range(tiles):
        pair_copy(last, j).wait()
        value = total[2 * last + 1, j] + pair_in[last, j]
        for at in range(last):
            line_copy(at, j).wait()
            value = value + line_in[at, j].astype(jnp.float32)
        grad_ref[:, :, j * tile : (j + 1) * tile] = value.astype(grad_ref.dtype).reshape(
            2, BLOCK, tile
        )
    start_all(to_head, own_head, 3, grad_ref, gc)

    scale = HD ** (-0.5)
    contract_last = (((1,), (1,)), ((), ()))
    wait_all(to_head, own_head, *attention[0])
    wait_all(to_head, own_head, *attention[1])
    for b in range(blocks):
        here = slice(b * BLOCK, (b + 1) * BLOCK)
        rows = kc[holder[b]]
        keys[here, :] = rows
        keys_t[:, here] = rows.T

    def pair(ref, i):
        return jnp.concatenate([ref[holder[2 * i]], ref[holder[2 * i + 1]]], axis=0)

    def add(sums, value, i):
        value = value.reshape(2 * i + 2, BLOCK, HD)
        if i == blocks // 2 - 1:
            sums[...] = value
        else:
            sums[: 2 * i + 2] += value

    def stored(i):
        return slice(tile * i * (i + 1) // 2, tile * (i + 1) * (i + 2) // 2)

    def give(sums, factor, low):
        for s in range(blocks):
            rows = sums[order_ref[s]]
            rows = rows if factor is None else rows * factor
            low[s] = rows.astype(low.dtype)

    for i in reversed(range(blocks // 2)):
        depth = (i + 1) * tile
        scores = lax.dot_general(
            keys[:depth, :], pair(qc, i), contract_last, preferred_element_type=jnp.float32
        ) * scale
        key_at = lax.broadcasted_iota(jnp.int32, (tile, tile), 0)
        query_at = lax.broadcasted_iota(jnp.int32, (tile, tile), 1)
        edge = jnp.where(key_at <= query_at, scores[depth - tile :], -1e30)
        scores = jnp.concatenate([scores[: depth - tile], edge], axis=0) if i else edge
        terms = jnp.exp(scores - jnp.max(scores, axis=0, keepdims=True))
        prob[stored(i), :] = terms * (1.0 / jnp.sum(terms, axis=0, keepdims=True))

    wait_all(to_head, own_head, 3, grad_ref, gc)
    for i in reversed(range(blocks // 2)):
        chance = prob[stored(i), :].astype(jnp.bfloat16)
        add(dv_sum, jnp.dot(chance, pair(gc, i), preferred_element_type=jnp.float32), i)
    give(dv_sum, None, dv_low)
    start_all(to_rows, own_rows, 4, dv_low, dv_ref)
    wait_all(to_head, own_head, *attention[2])
    for b in range(blocks):
        values[b * BLOCK : (b + 1) * BLOCK, :] = vc[holder[b]]
    for i in reversed(range(blocks // 2)):
        depth = (i + 1) * tile
        prob_grad = lax.dot_general(
            values[:depth, :], pair(gc, i), contract_last, preferred_element_type=jnp.float32
        )
        chance = prob[stored(i), :]
        delta = jnp.sum(chance * prob_grad, axis=0, keepdims=True)
        score_grad = (chance * (prob_grad - delta)).astype(jnp.bfloat16)
        add(dk_sum, jnp.dot(score_grad, pair(qc, i), preferred_element_type=jnp.float32), i)
        query_t = jnp.dot(keys_t[:, :depth], score_grad, preferred_element_type=jnp.float32)
        dq_sum[2 * i : 2 * i + 2] = (query_t.T * scale).reshape(2, BLOCK, HD)
    give(dq_sum, None, dq_low)
    start_all(to_rows, own_rows, 5, dq_low, dq_ref)
    give(dk_sum, scale, dk_low)
    start_all(to_rows, own_rows, 6, dk_low, dk_ref)
    wait_all(to_rows, own_rows, 4, dv_low, dv_ref)
    wait_all(to_rows, own_rows, 5, dq_low, dq_ref)
    wait_all(to_rows, own_rows, 6, dk_low, dk_ref)


def fused(n, heads, slots, collective, order, filters, *tensors):
    rows, width = tensors[0].shape
    weight = tensors[-1]
    blocks = order.shape[0]
    held = blocks // 2
    chips = heads // 2
    part = width // (n // 2)
    groups = part // GROUP
    tile = 2 * BLOCK
    tiles = width // tile
    stored = tile * (blocks // 2) * (blocks // 2 + 1) // 2
    bf16 = jnp.bfloat16
    local = pltpu.VMEM((2, BLOCK, width), bf16)
    mine = pltpu.VMEM((held, BLOCK, part), bf16)
    few = pltpu.VMEM((slots, BLOCK, part), bf16)
    table = pltpu.VMEM((2 * BLOCK, groups * 2 * BLOCK), bf16)
    column = pltpu.VMEM((blocks, BLOCK, HD), bf16)
    sums = pltpu.VMEM((blocks, BLOCK, HD), jnp.float32)
    dma = pltpu.SemaphoreType.DMA
    like = jax.ShapeDtypeStruct((2, BLOCK, width), bf16)
    return pl.pallas_call(
        functools.partial(fused_kernel, n, heads, slots),
        out_shape=[like] * 4,
        in_specs=[SMEM_SPEC, VMEM_SPEC] + [ANY_SPEC] * 8,
        out_specs=[VMEM_SPEC] * 4,
        scratch_shapes=[local] * 9
        + [mine] * 2
        + [few] * 4
        + [table] * 2
        + [mine] * 2
        + [local] * 2
        + [pltpu.VMEM((3, rows, width), bf16), pltpu.VMEM((2,) + weight.shape[1:], bf16)]
        + [
            pltpu.VMEM((2 * chips, tiles, rows, tile), jnp.float32),
            pltpu.VMEM((chips, tiles, rows, tile), jnp.float32),
            pltpu.VMEM((chips - 1, tiles, rows, tile), bf16),
            pltpu.VMEM((chips - 1, tiles, rows, tile), bf16),
        ]
        + [column] * 4
        + [
            pltpu.VMEM((blocks * BLOCK, HD), bf16),
            pltpu.VMEM((HD, blocks * BLOCK), bf16),
            pltpu.VMEM((blocks * BLOCK, HD), bf16),
            pltpu.VMEM((stored, tile), jnp.float32),
        ]
        + [sums] * 3
        + [column] * 3
        + [pltpu.SMEM((blocks,), jnp.int32)] * 7
        + [pltpu.SMEM((slots,), jnp.int32)] * 2
        + [
            dma((7,)), dma((3,)), dma((7,)), dma((7, n)), dma((7, n)),
            dma((4, n // 2)), dma((4, n // 2)), dma((4,)), dma((2,)), dma((2,)),
            dma((2, chips, tiles)), dma((2, chips, tiles)),
        ],
        compiler_params=pltpu.CompilerParams(
            collective_id=collective, has_side_effects=True, vmem_limit_bytes=61 * 2**20
        ),
    )(order, filters, *[t.reshape(2, BLOCK, width) for t in tensors[:-1]], weight)


def land_kernel(count, *refs):
    copies = [
        pltpu.make_async_copy(source, target, refs[-1].at[i])
        for i, (source, target) in enumerate(zip(refs[:count], refs[count:-1]))
    ]
    for copy in copies:
        copy.start()
    for copy in copies:
        copy.wait()


def land(*arrays):
    count = len(arrays)
    return pl.pallas_call(
        functools.partial(land_kernel, count),
        out_shape=[jax.ShapeDtypeStruct(a.shape, a.dtype) for a in arrays],
        in_specs=[VMEM_SPEC] * count,
        out_specs=[ANY_SPEC] * count,
        scratch_shapes=[pltpu.SemaphoreType.DMA((count,))],
        compiler_params=pltpu.CompilerParams(vmem_limit_bytes=2**20),
    )(*arrays)


def column_device(
    block_order, queries, keys, values, hyena_q, hyena_k, hyena_v, hyena_grad, filters, proj_weight
):
    n = lax.axis_size("seq")
    heads = lax.axis_size("head")
    held = block_order.shape[0] // 2
    grads = fused(
        n, heads, held, 0, block_order, filters,
        hyena_q, hyena_k, hyena_v, hyena_grad, queries, keys, values, proj_weight,
    )
    return tuple(out.reshape(queries.shape) for out in land(*grads))


def per_device(*arrays):
    queries, filters = arrays[1], arrays[8]
    n = lax.axis_size("seq")
    whole_heads = queries.shape[1] == n * HD and queries.shape[0] == 2 * BLOCK
    paired = lax.axis_size("head") % 2 == 0 and lax.axis_size("head") > 2
    split = n % 4 == 0 and filters.shape[0] % (8 * n) == 0
    if whole_heads and paired and split and KL == BLOCK == HD:
        return column_device(*arrays)
    return ring_device(*arrays)


def solution(mesh):
    placed = (
        P(),
        P("seq", "head"),
        P("seq", "head"),
        P("seq", "head"),
        P("seq", "head"),
        P("seq", "head"),
        P("seq", "head"),
        P("seq", "head"),
        P("head", None),
        P(None, None, "head"),
    )
    return jax.shard_map(
        per_device,
        mesh=mesh,
        in_specs=placed,
        out_specs=(P("seq", "head"), P("seq", "head"), P("seq", "head"), P("seq", "head")),
        check_vma=False,
    )
```

time: 170 us -> 154 us (0.906)
  Pallas kernels: 158 us -> 149 us
  local copies, waits for them, and re-layouts: 8.32 us -> 4.16 us
  other arithmetic: 2.25 us -> 0 us
    pallas_call x2 -> x1, Pallas kernels: 155 us -> 147 us  [fused(): pl.pallas_call(functools.partial(fused_kernel, n, heads, slots), out_shap...]
    unnamed x18 -> x8, local copies, waits for them, and re-layouts: 6.55 us -> 4.16 us
where the time goes in v1:
time: 154 us
  Pallas kernels  149 us (97%)
  local copies, waits for them, and re-layouts  4.16 us (3%)
    pallas_call x1, Pallas kernels, fused(): pl.pallas_call(functools.partial(fused_kernel, n, heads, slots), out_shap...  147 us
    unnamed x8, local copies, waits for them, and re-layouts  4.16 us

profile of v1, /device:TPU:0, one launch (start us, length us, event | category | flops | bytes accessed | tf_op | source)
XLA Modules:
  0.0 153.7 jit_solution(9626619686187614562)
XLA Ops:
  0.6 147.4 %shard_map.129 = (bf16[2,128,1024]{2,1,0:T(8,128)(2,1)}, bf16[2,128,1024]{2,1,0:T(8,128)(2,1)}, bf16[2,128,1024]{2,1,0:T(8,128)(2,1)}, bf16[2,128,1024]{2,1,0:T(8,128)(2,1)}) custom-call(s32[16]{0:T(128)} %order_ref.1, f32[64,128]{1,0:T(8,128)} %filters_ref.1, bf16[2,128,1024]{2,1,0:T(8,128)(2,1)} %bitcast.11, bf16[2,128,1024]{2,1,0:T(8,128)(2,1)} %bitcast.12, ...), custom_call_target="tpu_custom_call" | custom-call | tf_op jit(solution)/shard_map/pallas_call | solution.py:684
  148.0 0.0 copy-start
  148.0 1.0 copy-done
  149.1 0.0 copy-start.1
  149.1 1.0 copy-done.1
  150.1 0.0 copy-start.2
  150.1 1.0 copy-done.2
  151.1 0.0 copy-start.3
  151.1 1.0 copy-done.3
  152.2 1.3 shard_map.130
Async XLA Ops:
  148.0 1.0 copy-start
  149.1 1.0 copy-start.1
  150.1 1.0 copy-start.2
  151.1 1.0 copy-start.3

commit v2 on v1

--- a/solution.py
+++ b/solution.py
@@ -246,6 +246,9 @@
 SMEM_SPEC = pl.BlockSpec(memory_space=pltpu.SMEM)
 
 
+LOG2E = 1.4426950408889634
+
+
 def aligned(index, size):
     return pl.ds(pl.multiple_of(index * size, size), size)
 
@@ -253,14 +256,14 @@
 def fused_kernel(
     n, heads, slots,
     order_ref, filters_ref, hq_in, hk_in, hv_in, hg_in, q_in, k_in, v_in, weight_in,
-    grad_ref, dq_ref, dk_ref, dv_ref,
-    hq, hk, hv, hg, qs, ks, vs, z_own, dc_own,
+    grad_out, dq_ref, dk_ref, dv_ref,
+    hq, hk, hv, hg, qs, ks, vs, z_own, dc_own, grad_ref,
     zc, dcc, z_out, dc_out, z_far, dc_far,
-    causal, anti, convc, dzc, conv, dz, stacked, weights,
+    lines, causal, anti, convc, dzc, conv, dz, stacked, weights,
     total, pair_in, line_out, line_in,
-    qc, kc, vc, gc, keys, keys_t, values, prob, dq_sum, dk_sum, dv_sum, dq_low, dk_low, dv_low,
+    qc, kc, vc, gc, keys, keys_t, values, prob, inverse, dq_sum, dk_sum, dv_sum, dq_low, dk_low, dv_low,
     holder, after, before, z_cross, dc_cross, z_rank, dc_rank, z_pick, dc_pick,
-    load_sem, weight_sem, own_sem, send_sem, recv_sem,
+    load_sem, weight_sem, last_sem, own_sem, send_sem, recv_sem,
     half_send, half_recv, half_own, far_send, far_recv, pair_sem, line_sem,
 ):
     me = lax.axis_index("seq")
@@ -293,9 +296,6 @@
     def weight_copy(m, slot):
         return pltpu.make_async_copy(weight_in.at[m], weights.at[slot], weight_sem.at[m])
 
-    weight_copy(1, 0).start()
-    weight_copy(2, 1).start()
-
     barrier = pltpu.get_barrier_semaphore()
     for step in range(1, n):
         pl.semaphore_signal(
@@ -314,10 +314,20 @@
     loads[2].wait()
     loads[3].wait()
     z_own[...] = (wide_of(hk) * wide_of(hv)).astype(jnp.bfloat16)
+    weight_copy(1, 0).start()
+    weight_copy(2, 1).start()
     pl.semaphore_wait(barrier, n - 1 + len(head_peers))
 
+    far_steps, near_steps = list(range(members)), list(range(members + 1, n))
+    mixed = [s for both in zip(far_steps, near_steps) for s in both] + far_steps[len(near_steps) :]
+
+    def peer_at(step):
+        if step < members:
+            return (1 - side) * members + lax.rem(place + step, members)
+        return side * members + lax.rem(place + step - members, members)
+
     def to_head(tensor, src, dst, step):
-        peer = lax.rem(me + step, n)
+        peer = peer_at(step)
         return pltpu.make_async_remote_copy(
             src_ref=src.at[:, :, aligned(peer, HD)], dst_ref=dst.at[aligned(me, 2)],
             send_sem=send_sem.at[tensor, step], recv_sem=recv_sem.at[tensor, step],
@@ -325,7 +335,7 @@
         )
 
     def to_rows(tensor, src, dst, step):
-        peer = lax.rem(me + step, n)
+        peer = peer_at(step)
         return pltpu.make_async_remote_copy(
             src_ref=src.at[aligned(peer, 2)], dst_ref=dst.at[:, :, aligned(me, HD)],
             send_sem=send_sem.at[tensor, step], recv_sem=recv_sem.at[tensor, step],
@@ -343,12 +353,12 @@
         )
 
     def start_all(make, own, tensor, src, dst):
-        for step in range(1, n):
+        for step in mixed:
             make(tensor, src, dst, step).start()
         own(tensor, src, dst).start()
 
     def wait_all(make, own, tensor, src, dst):
-        for step in range(1, n):
+        for step in mixed:
             make(tensor, src, dst, step).wait()
         own(tensor, src, dst).wait()
 
@@ -389,6 +399,14 @@
         for step in range(1, members):
             spread(tensor, src, dst, step).start()
         spread_own(tensor, src, dst).start()
+    loads[4].wait()
+    loads[5].wait()
+    inner = place // (members // 2) != side
+
+    @pl.when(inner)
+    def _():
+        for step in far_steps:
+            to_head(0, qs, qc, step).start()
 
     order = [order_ref[r] for r in range(blocks)]
     for p in range(blocks):
@@ -420,6 +438,15 @@
                 found = jnp.where((flags[l] == 1) & (ranks[l] == k), l, found)
             pick[k] = found
 
+    for tensor, src, dst, pick, out, far in (
+        (0, dc_own, dcc, dc_pick, dc_out, dc_far), (1, z_own, zc, z_pick, z_out, z_far)
+    ):
+        for step in range(1, members):
+            spread(tensor, src, dst, step).wait()
+        spread_own(tensor, src, dst).wait()
+        for k in range(slots):
+            out[k] = dst[pick[k]]
+        cross(tensor, out, far).start()
     window = 2 * BLOCK
     taps = filters_ref[aligned(place, groups), :]
     flip = jnp.where(
@@ -430,26 +457,20 @@
     low = (taps - high.astype(jnp.float32)).astype(jnp.bfloat16)
     turned = jnp.dot(high, flip, preferred_element_type=jnp.float32)
     turned = turned + jnp.dot(low, flip, preferred_element_type=jnp.float32)
-    for table, rows, shift in ((anti, taps, 0), (causal, turned, 1)):
-        padded = jnp.concatenate([rows, jnp.zeros_like(rows)], axis=1)
-        for g in range(groups):
-            line = jnp.broadcast_to(padded[g : g + 1, :], (BLOCK, window))
-            line = pltpu.roll(line, shift, 1, stride=1, stride_axis=0)
+    for at, rows in ((0, taps), (1, turned)):
+        lines[at] = jnp.concatenate([rows, jnp.zeros_like(rows)], axis=1)
+
+    def build(g, carry):
+        lanes = aligned(g, window)
+        for at, table in ((0, anti), (1, causal)):
+            line = jnp.broadcast_to(lines[at, pl.ds(g, 1), :], (BLOCK, window))
+            line = pltpu.roll(line, at, 1, stride=1, stride_axis=0)
             top = line.astype(jnp.bfloat16)
-            table[:BLOCK, g * window : (g + 1) * window] = top
-            table[BLOCK:, g * window : (g + 1) * window] = (
-                line - top.astype(jnp.float32)
-            ).astype(jnp.bfloat16)
-
-    for tensor, src, dst, pick, out, far in (
-        (0, dc_own, dcc, dc_pick, dc_out, dc_far), (1, z_own, zc, z_pick, z_out, z_far)
-    ):
-        for step in range(1, members):
-            spread(tensor, src, dst, step).wait()
-        spread_own(tensor, src, dst).wait()
-        for k in range(slots):
-            out[k] = dst[pick[k]]
-        cross(tensor, out, far).start()
+            table[:BLOCK, lanes] = top
+            table[BLOCK:, lanes] = (line - top.astype(jnp.float32)).astype(jnp.bfloat16)
+        return carry
+
+    lax.fori_loop(0, groups, build, 0)
 
     lane_group = lax.broadcasted_iota(jnp.int32, (window, window), 1) % HD // GROUP
     chunks = part // HD
@@ -494,11 +515,14 @@
         def one(step, carry):
             goal = lax.rem(place + step, members)
             filtered(goal, near, far, linked, end, rank, table, target, own_first)
-            collect(tensor, target, out, step).start()
+
+            @pl.when(step < members)
+            def _():
+                collect(tensor, target, out, step).start()
+
             return carry
 
-        lax.fori_loop(1, members, one, 0)
-        filtered(place, near, far, linked, end, rank, table, target, own_first)
+        lax.fori_loop(1, members + 1, one, 0)
         collect_own(tensor, target, out).start()
 
     def returned(tensor, target, out):
@@ -512,16 +536,41 @@
     cross(0, dc_out, dc_far).wait()
     send_back(2, dcc, dc_far, after, blocks - 1, dc_rank, anti, dzc, dz, True)
     cross(1, z_out, z_far).wait()
+
+    @pl.when(inner)
+    def _():
+        for step in far_steps:
+            to_head(1, ks, kc, step).start()
+
     send_back(3, zc, z_far, before, 0, z_rank, causal, convc, conv, False)
     attention = ((0, qs, qc), (1, ks, kc), (2, vs, vc))
-    for t, src, dst in attention:
-        loads[4 + t].wait()
-        start_all(to_head, own_head, t, src, dst)
+
+    @pl.when(jnp.logical_not(inner))
+    def _():
+        for step in far_steps:
+            to_head(0, qs, qc, step).start()
+        for step in far_steps:
+            to_head(1, ks, kc, step).start()
+
+    for step in near_steps:
+        to_head(0, qs, qc, step).start()
+    own_head(0, qs, qc).start()
+    for step in near_steps:
+        to_head(1, ks, kc, step).start()
+    own_head(1, ks, kc).start()
+    loads[6].wait()
+    start_all(to_head, own_head, *attention[2])
 
     goals = []
     for step in steps:
         goals.append(along[step] * 2 + 1 - core)
         goals.append(along[step] * 2 + core)
+
+    def last_weight(slot):
+        rows = aligned(goals[slot], width)
+        return pltpu.make_async_copy(
+            weight_in.at[0, rows], weights.at[0, rows], last_sem.at[slot]
+        )
 
     def product(m, slot, goal, j):
         return lax.dot_general(
@@ -541,10 +590,9 @@
             return carry
 
         lax.fori_loop(0, tiles, begin, 0)
-    weight_copy(0, 0).start()
+        last_weight(slot).start()
     returned(3, convc, conv)
     stacked[0] = rows_of((wide_of(hg) * wide_of(conv)).astype(jnp.bfloat16))
-    weight_copy(0, 0).wait()
 
     def pair_copy(at, j):
         return pltpu.make_async_remote_copy(
@@ -561,12 +609,15 @@
         )
 
     for at in range(chips):
+        last_weight(2 * at).wait()
+
         def give_pair(j, carry, at=at):
             total[2 * at, j] += product(0, 0, goals[2 * at], j)
             pair_copy(at, j).start()
             return carry
 
         lax.fori_loop(0, tiles, give_pair, 0)
+        last_weight(2 * at + 1).wait()
 
         def keep(j, carry, at=at):
             value = total[2 * at + 1, j] + product(0, 0, goals[2 * at + 1], j)
@@ -590,6 +641,8 @@
             2, BLOCK, tile
         )
     start_all(to_head, own_head, 3, grad_ref, gc)
+    grad_copy = pltpu.make_async_copy(grad_ref, grad_out, load_sem.at[7])
+    grad_copy.start()
 
     scale = HD ** (-0.5)
     contract_last = (((1,), (1,)), ((), ()))
@@ -611,8 +664,10 @@
         else:
             sums[: 2 * i + 2] += value
 
-    def stored(i):
-        return slice(tile * i * (i + 1) // 2, tile * (i + 1) * (i + 2) // 2)
+    def chance_of(i):
+        first = i * (i + 1) // 2
+        terms = prob[first : first + i + 1].reshape((i + 1) * tile, tile)
+        return terms * inverse[i]
 
     def give(sums, factor, low):
         for s in range(blocks):
@@ -620,21 +675,48 @@
             rows = rows if factor is None else rows * factor
             low[s] = rows.astype(low.dtype)
 
-    for i in reversed(range(blocks // 2)):
-        depth = (i + 1) * tile
-        scores = lax.dot_general(
-            keys[:depth, :], pair(qc, i), contract_last, preferred_element_type=jnp.float32
-        ) * scale
-        key_at = lax.broadcasted_iota(jnp.int32, (tile, tile), 0)
-        query_at = lax.broadcasted_iota(jnp.int32, (tile, tile), 1)
-        edge = jnp.where(key_at <= query_at, scores[depth - tile :], -1e30)
-        scores = jnp.concatenate([scores[: depth - tile], edge], axis=0) if i else edge
-        terms = jnp.exp(scores - jnp.max(scores, axis=0, keepdims=True))
-        prob[stored(i), :] = terms * (1.0 / jnp.sum(terms, axis=0, keepdims=True))
+    key_at = lax.broadcasted_iota(jnp.int32, (tile, tile), 0)
+    query_at = lax.broadcasted_iota(jnp.int32, (tile, tile), 1)
+    rate = scale * LOG2E
+
+    def folded(value, op):
+        value = value.reshape(tile // 8, 8, tile)
+        return op(value, axis=0)
+
+    def chances(i, carry):
+        q = pair(qc, i)
+        first = i * (i + 1) // 2
+
+        def score(j, top):
+            value = lax.dot_general(
+                keys[aligned(j, tile), :], q, contract_last, preferred_element_type=jnp.float32
+            )
+            prob[first + j] = value
+            return jnp.maximum(top, folded(value, jnp.max))
+
+        top = lax.fori_loop(0, i, score, jnp.full((8, tile), -1e30, jnp.float32))
+        value = lax.dot_general(
+            keys[aligned(i, tile), :], q, contract_last, preferred_element_type=jnp.float32
+        )
+        value = jnp.where(key_at <= query_at, value, -1e30)
+        prob[first + i] = value
+        top = jnp.maximum(top, folded(value, jnp.max))
+        top = jnp.max(top, axis=0, keepdims=True)
+
+        def term(j, sums):
+            value = jnp.exp2((prob[first + j] - top) * rate)
+            prob[first + j] = value
+            return sums + folded(value, jnp.sum)
+
+        sums = lax.fori_loop(0, i + 1, term, jnp.zeros((8, tile), jnp.float32))
+        inverse[i] = 1.0 / jnp.sum(sums, axis=0, keepdims=True)
+        return carry
+
+    lax.fori_loop(0, blocks // 2, chances, 0)
 
     wait_all(to_head, own_head, 3, grad_ref, gc)
     for i in reversed(range(blocks // 2)):
-        chance = prob[stored(i), :].astype(jnp.bfloat16)
+        chance = chance_of(i).astype(jnp.bfloat16)
         add(dv_sum, jnp.dot(chance, pair(gc, i), preferred_element_type=jnp.float32), i)
     give(dv_sum, None, dv_low)
     start_all(to_rows, own_rows, 4, dv_low, dv_ref)
@@ -646,7 +728,7 @@
         prob_grad = lax.dot_general(
             values[:depth, :], pair(gc, i), contract_last, preferred_element_type=jnp.float32
         )
-        chance = prob[stored(i), :]
+        chance = chance_of(i)
         delta = jnp.sum(chance * prob_grad, axis=0, keepdims=True)
         score_grad = (chance * (prob_grad - delta)).astype(jnp.bfloat16)
         add(dk_sum, jnp.dot(score_grad, pair(qc, i), preferred_element_type=jnp.float32), i)
@@ -656,6 +738,7 @@
     start_all(to_rows, own_rows, 5, dq_low, dq_ref)
     give(dk_sum, scale, dk_low)
     start_all(to_rows, own_rows, 6, dk_low, dk_ref)
+    grad_copy.wait()
     wait_all(to_rows, own_rows, 4, dv_low, dv_ref)
     wait_all(to_rows, own_rows, 5, dq_low, dq_ref)
     wait_all(to_rows, own_rows, 6, dk_low, dk_ref)
@@ -671,7 +754,7 @@
     groups = part // GROUP
     tile = 2 * BLOCK
     tiles = width // tile
-    stored = tile * (blocks // 2) * (blocks // 2 + 1) // 2
+    stored = (blocks // 2) * (blocks // 2 + 1) // 2
     bf16 = jnp.bfloat16
     local = pltpu.VMEM((2, BLOCK, width), bf16)
     mine = pltpu.VMEM((held, BLOCK, part), bf16)
@@ -685,10 +768,11 @@
         functools.partial(fused_kernel, n, heads, slots),
         out_shape=[like] * 4,
         in_specs=[SMEM_SPEC, VMEM_SPEC] + [ANY_SPEC] * 8,
-        out_specs=[VMEM_SPEC] * 4,
-        scratch_shapes=[local] * 9
+        out_specs=[ANY_SPEC] * 4,
+        scratch_shapes=[local] * 10
         + [mine] * 2
         + [few] * 4
+        + [pltpu.VMEM((2, groups, 2 * BLOCK), jnp.float32)]
         + [table] * 2
         + [mine] * 2
         + [local] * 2
@@ -704,31 +788,35 @@
             pltpu.VMEM((blocks * BLOCK, HD), bf16),
             pltpu.VMEM((HD, blocks * BLOCK), bf16),
             pltpu.VMEM((blocks * BLOCK, HD), bf16),
-            pltpu.VMEM((stored, tile), jnp.float32),
+            pltpu.VMEM((stored, tile, tile), jnp.float32),
+            pltpu.VMEM((blocks // 2, 1, tile), jnp.float32),
         ]
         + [sums] * 3
         + [column] * 3
         + [pltpu.SMEM((blocks,), jnp.int32)] * 7
         + [pltpu.SMEM((slots,), jnp.int32)] * 2
         + [
-            dma((7,)), dma((3,)), dma((7,)), dma((7, n)), dma((7, n)),
+            dma((8,)), dma((3,)), dma((heads,)), dma((7,)), dma((7, n)), dma((7, n)),
             dma((4, n // 2)), dma((4, n // 2)), dma((4,)), dma((2,)), dma((2,)),
             dma((2, chips, tiles)), dma((2, chips, tiles)),
         ],
         compiler_params=pltpu.CompilerParams(
-            collective_id=collective, has_side_effects=True, vmem_limit_bytes=61 * 2**20
+            collective_id=collective, has_side_effects=True, vmem_limit_bytes=63 * 2**20
         ),
     )(order, filters, *[t.reshape(2, BLOCK, width) for t in tensors[:-1]], weight)
 
 
 def land_kernel(count, *refs):
-    copies = [
-        pltpu.make_async_copy(source, target, refs[-1].at[i])
-        for i, (source, target) in enumerate(zip(refs[:count], refs[count:-1]))
-    ]
-    for copy in copies:
+    sources, targets, held = refs[:count], refs[count : 2 * count], refs[2 * count : 3 * count]
+    take, put = refs[3 * count :]
+    arrive = [pltpu.make_async_copy(sources[i], held[i], take.at[i]) for i in range(count)]
+    leave = [pltpu.make_async_copy(held[i], targets[i], put.at[i]) for i in range(count)]
+    for copy in arrive:
         copy.start()
-    for copy in copies:
+    for i in range(count):
+        arrive[i].wait()
+        leave[i].start()
+    for copy in leave:
         copy.wait()
 
 
@@ -737,10 +825,10 @@
     return pl.pallas_call(
         functools.partial(land_kernel, count),
         out_shape=[jax.ShapeDtypeStruct(a.shape, a.dtype) for a in arrays],
-        in_specs=[VMEM_SPEC] * count,
+        in_specs=[ANY_SPEC] * count,
         out_specs=[ANY_SPEC] * count,
-        scratch_shapes=[pltpu.SemaphoreType.DMA((count,))],
-        compiler_params=pltpu.CompilerParams(vmem_limit_bytes=2**20),
+        scratch_shapes=[pltpu.VMEM(a.shape, a.dtype) for a in arrays]
+        + [pltpu.SemaphoreType.DMA((count,))] * 2,
     )(*arrays)
 
 
@@ -750,11 +838,25 @@
     n = lax.axis_size("seq")
     heads = lax.axis_size("head")
     held = block_order.shape[0] // 2
-    grads = fused(
-        n, heads, held, 0, block_order, filters,
+    few = held // 2 + 1
+    follows = block_order[None, :] == block_order[:, None] + 1
+    ids = jnp.arange(2 * held, dtype=jnp.int32)
+    first = ids < held
+    leaving = jnp.sum(follows & first[:, None] & ~first[None, :], dtype=jnp.int32)
+    coming = jnp.sum(follows & ~first[:, None] & first[None, :], dtype=jnp.int32)
+    fits = jnp.maximum(leaving, coming) <= few
+
+    def run(slots, collective):
+        def call(*arrays):
+            return tuple(land(*fused(n, heads, slots, collective, *arrays)))
+
+        return call
+
+    grads = lax.cond(
+        fits, run(few, 0), run(held, 1), block_order, filters,
         hyena_q, hyena_k, hyena_v, hyena_grad, queries, keys, values, proj_weight,
     )
-    return tuple(out.reshape(queries.shape) for out in land(*grads))
+    return tuple(out.reshape(queries.shape) for out in grads)
 
 
 def per_device(*arrays):

time: 154 us -> 139 us (0.903)
  Pallas kernels: 149 us -> 134 us
  local copies, waits for them, and re-layouts: 4.16 us -> 0 us
  other arithmetic: 0 us -> 2.04 us
    pallas_call x1, Pallas kernels: 147 us -> 132 us  [fused(): pl.pallas_call(functools.partial(fused_kernel, n, heads, slots), out_shap...]
    unnamed x8 -> x0, local copies, waits for them, and re-layouts: 4.16 us -> none
where the time goes in v2:
time: 139 us
  Pallas kernels  134 us (96%)
  between operations  2.11 us (2%)
  other arithmetic  2.04 us (1%)
    pallas_call x1, Pallas kernels, fused(): pl.pallas_call(functools.partial(fused_kernel, n, heads, slots), out_shap...  132 us

profile of v2, /device:TPU:0, one launch (start us, length us, event | category | flops | bytes accessed | tf_op | source)
XLA Modules:
  0.0 138.7 jit_solution(6376618837958746369)
XLA Ops:
  0.6 0.7 broadcast_add_fusion
  1.3 1.4 convert_reduce_fusion
  4.0 134.5 %conditional.1 = ((bf16[2,128,1024]{2,1,0:T(8,128)(2,1)}, bf16[2,128,1024]{2,1,0:T(8,128)(2,1)}, bf16[2,128,1024]{2,1,0:T(8,128)(2,1)}, bf16[2,128,1024]{2,1,0:T(8,128)(2,1)})) conditional(s32[]{:T(128)} %convert_element_type.11, (bf16[256,1024]{1,0:T(8,128)(2,1)}, bf16[256,1024]{1,0:T(8,128)(2,1)}, bf16[256,1024]{1,0:T(8,128)(2,1)}, ...), branch_computations={%region_2.0_spmd.clone, %region_3.0_spmd.clone} | conditional | bytes 8 | solution.py:855
  4.2 131.8 %branch_1_fun.2 = (bf16[2,128,1024]{2,1,0:T(8,128)(2,1)}, bf16[2,128,1024]{2,1,0:T(8,128)(2,1)}, bf16[2,128,1024]{2,1,0:T(8,128)(2,1)}, bf16[2,128,1024]{2,1,0:T(8,128)(2,1)}) custom-call(s32[16]{0:T(128)} %get-tuple-element.113.order_ref, f32[64,128]{1,0:T(8,128)} %get-tuple-element.114.filters_ref, bf16[2,128,1024]{2,1,0:T(8,128)(2,1)} %bitcast.19, ...), custom_call_target="tpu_custom_call" | custom-call | tf_op jit(solution)/shard_map/cond/branch_1_fun/pallas_call | solution.py:767
  136.1 2.4 %branch_1_fun.3 = (bf16[2,128,1024]{2,1,0:T(8,128)(2,1)}, bf16[2,128,1024]{2,1,0:T(8,128)(2,1)}, bf16[2,128,1024]{2,1,0:T(8,128)(2,1)}, bf16[2,128,1024]{2,1,0:T(8,128)(2,1)}) custom-call(bf16[2,128,1024]{2,1,0:T(8,128)(2,1)} %get-tuple-element.123.refs_0_, bf16[2,128,1024]{2,1,0:T(8,128)(2,1)} %get-tuple-element.124.refs_1_, ...), custom_call_target="tpu_custom_call" | custom-call | tf_op jit(solution)/shard_map/cond/branch_1_fun/pallas_call | solution.py:825
  (1 shorter events, 0.0 us)

commit v3 on v2

--- a/solution.py
+++ b/solution.py
@@ -406,6 +406,11 @@
     @pl.when(inner)
     def _():
         for step in far_steps:
+            to_head(0, qs, qc, step).start()
+
+    @pl.when(jnp.logical_not(inner))
+    def _():
+        for step in near_steps:
             to_head(0, qs, qc, step).start()
 
     order = [order_ref[r] for r in range(blocks)]
@@ -542,18 +547,24 @@
         for step in far_steps:
             to_head(1, ks, kc, step).start()
 
-    send_back(3, zc, z_far, before, 0, z_rank, causal, convc, conv, False)
-    attention = ((0, qs, qc), (1, ks, kc), (2, vs, vc))
-
     @pl.when(jnp.logical_not(inner))
     def _():
         for step in far_steps:
             to_head(0, qs, qc, step).start()
+
+    send_back(3, zc, z_far, before, 0, z_rank, causal, convc, conv, False)
+    attention = ((0, qs, qc), (1, ks, kc), (2, vs, vc))
+
+    @pl.when(inner)
+    def _():
+        for step in near_steps:
+            to_head(0, qs, qc, step).start()
+
+    @pl.when(jnp.logical_not(inner))
+    def _():
         for step in far_steps:
             to_head(1, ks, kc, step).start()
 
-    for step in near_steps:
-        to_head(0, qs, qc, step).start()
     own_head(0, qs, qc).start()
     for step in near_steps:
         to_head(1, ks, kc, step).start()
@@ -839,12 +850,10 @@
     heads = lax.axis_size("head")
     held = block_order.shape[0] // 2
     few = held // 2 + 1
+    ids = jnp.arange(2 * held, dtype=jnp.int32)
     follows = block_order[None, :] == block_order[:, None] + 1
-    ids = jnp.arange(2 * held, dtype=jnp.int32)
-    first = ids < held
-    leaving = jnp.sum(follows & first[:, None] & ~first[None, :], dtype=jnp.int32)
-    coming = jnp.sum(follows & ~first[:, None] & first[None, :], dtype=jnp.int32)
-    fits = jnp.maximum(leaving, coming) <= few
+    parted = (ids[None, :] < held) != (ids[:, None] < held)
+    fits = jnp.sum((follows & parted).astype(jnp.int32)) <= 2 * few
 
     def run(slots, collective):
         def call(*arrays):

time: 139 us -> 142 us (1.022)
  Pallas kernels: 134 us -> 138 us
    pallas_call x1, Pallas kernels: 132 us -> 135 us  [fused(): pl.pallas_call(functools.partial(fused_kernel, n, heads, slots), out_shap...]
where the time goes in v3:
time: 142 us
  Pallas kernels  138 us (97%)
  other arithmetic  2.03 us (1%)
  between operations  1.51 us (1%)
    pallas_call x1, Pallas kernels, fused(): pl.pallas_call(functools.partial(fused_kernel, n, heads, slots), out_shap...  135 us

profile of v3, /device:TPU:0, one launch (start us, length us, event | category | flops | bytes accessed | tf_op | source)
XLA Modules:
  0.0 142.0 jit_solution(14070534233735185710)
XLA Ops:
  0.6 0.7 broadcast_add_fusion
  1.3 1.4 convert_reduce_fusion
  3.3 138.4 %conditional.1 = ((bf16[2,128,1024]{2,1,0:T(8,128)(2,1)}, bf16[2,128,1024]{2,1,0:T(8,128)(2,1)}, bf16[2,128,1024]{2,1,0:T(8,128)(2,1)}, bf16[2,128,1024]{2,1,0:T(8,128)(2,1)})) conditional(s32[]{:T(128)} %convert_element_type.7, (bf16[256,1024]{1,0:T(8,128)(2,1)}, bf16[256,1024]{1,0:T(8,128)(2,1)}, bf16[256,1024]{1,0:T(8,128)(2,1)}, ...), branch_computations={%region_1.0_spmd.clone, %region_2.0_spmd.clone} | conditional | bytes 8 | solution.py:864
  3.6 135.5 %branch_1_fun.2 = (bf16[2,128,1024]{2,1,0:T(8,128)(2,1)}, bf16[2,128,1024]{2,1,0:T(8,128)(2,1)}, bf16[2,128,1024]{2,1,0:T(8,128)(2,1)}, bf16[2,128,1024]{2,1,0:T(8,128)(2,1)}) custom-call(s32[16]{0:T(128)} %get-tuple-element.113.order_ref, f32[64,128]{1,0:T(8,128)} %get-tuple-element.114.filters_ref, bf16[2,128,1024]{2,1,0:T(8,128)(2,1)} %bitcast.19, ...), custom_call_target="tpu_custom_call" | custom-call | tf_op jit(solution)/shard_map/cond/branch_1_fun/pallas_call | solution.py:778
  139.0 2.4 %branch_1_fun.3 = (bf16[2,128,1024]{2,1,0:T(8,128)(2,1)}, bf16[2,128,1024]{2,1,0:T(8,128)(2,1)}, bf16[2,128,1024]{2,1,0:T(8,128)(2,1)}, bf16[2,128,1024]{2,1,0:T(8,128)(2,1)}) custom-call(bf16[2,128,1024]{2,1,0:T(8,128)(2,1)} %get-tuple-element.123.refs_0_, bf16[2,128,1024]{2,1,0:T(8,128)(2,1)} %get-tuple-element.124.refs_1_, ...), custom_call_target="tpu_custom_call" | custom-call | tf_op jit(solution)/shard_map/cond/branch_1_fun/pallas_call | solution.py:836
  (1 shorter events, 0.0 us)
